TPU v7x, 32 devices: a whole 2x2x4 slice. The times are simulated.
32 devices in a mesh: lat: 4 (over y, core), lon: 8 (over z, x).
Axes of the slice: x: 2, y: 2, z: 4, core: 2. Of those that a mesh axis runs over, the one named last changes fastest.
Arguments:
- control: bfloat16 [80, 32, 64, 512], P(None, None, 'lon', 'lat'), may hold values from -6 to 6
- ensemble: bfloat16 [80, 32, 64, 512], P(None, None, 'lon', 'lat'), may hold values from -1.1953125 to 1.1953125
- level_mix: bfloat16 [32, 32], replicated, may hold values from -1 to 1
- lat_taps: float32 [4], replicated, may hold values from 0.1 to 0.6
- lon_taps: float32 [4], replicated, may hold values from 0.1 to 0.6
- obs_location: int32 [8, 4, 2048], P('lon', 'lat'), may hold values from 0 to 32767
- obs_count: int32 [8, 4], P('lon', 'lat'), may hold values from 512 to 2048, as said below
- obs_keep: int32 [8, 4, 2048], P('lon', 'lat'), may hold values 0 or 1
- innovation: float32 [8, 4, 2048], P('lon', 'lat'), may hold values from -6 to 6
- obs_weight: float32 [8, 4, 2048], P('lon', 'lat'), may hold values from 0.25 to 4
Outputs:
- gradient: float32 [80, 32, 64, 512], P(None, None, 'lon', 'lat')
- upper_factor: float32 [80, 80], replicated
Inputs may be any that keep to these rules, and one draw needn't show every extreme that they name: `obs_count`: live slots of a tile come first; some tile has all 2048 slots live.
All inputs are finite; a program needn't handle non-finite values. No bound on the sum of `obs_keep` on one device may be relied on, other than what follows from the above.
Results may differ from a plain program's by a relative error of at most 0.0028.
Values may be sent and summed in bfloat16 or wider, within the bound.
A program may use at most 128 MiB of HBM per device.

v0:
```python
import jax
import jax.numpy as jnp
import numpy as np
from jax import lax
from jax.experimental import pallas as pl
from jax.experimental.pallas import tpu as pltpu
from jax.sharding import PartitionSpec as P

OFFSETS = (-2, -1, 1, 2)
F32, BF = jnp.float32, jnp.bfloat16
VMEM_LIMIT = 56 * 1024 * 1024


def code_of(diff):
    out = np.zeros(diff.shape, np.int32)
    for t, offset in enumerate(OFFSETS):
        out[diff == offset] = t + 1
    out[diff == 0] = 5
    return out


def nn(a, b):
    return jnp.dot(a, b, preferred_element_type=F32)


def nt(a, b):
    return lax.dot_general(a, b, (((1,), (1,)), ((), ())), preferred_element_type=F32)


def tn(a, b):
    return lax.dot_general(a, b, (((0,), (0,)), ((), ())), preferred_element_type=F32)


def part3(x):
    a = x.astype(BF)
    r = x - a.astype(F32)
    b = r.astype(BF)
    c = (r - b.astype(F32)).astype(BF)
    return a, b, c


def setup_kernel(taps_ref, mix_ref, code_ref, codet_ref, ecode_ref, ecodet_ref, spread_ref, same_ref,
                 lf_ref, la_ref, bf_ref, ba_ref, xh_ref, xl_ref, kl_ref, klt_ref, xcode_ref):
    def put(code, base):
        out = jnp.where(code == 5, 1.0, 0.0)
        for t in range(4):
            out = out + jnp.where(code == t + 1, taps_ref[base + t], 0.0)
        hi = out.astype(BF)
        return hi, (out - hi.astype(F32)).astype(BF)

    lf_ref[...] = jnp.concatenate(put(code_ref[...], 0), axis=1)
    la_ref[...] = jnp.concatenate(put(codet_ref[...], 0), axis=1)
    hi, lo = put(ecode_ref[...], 0)
    top = lax.broadcasted_iota(jnp.int32, hi.shape, 0) < 4
    bf_ref[...] = jnp.where(top, hi.astype(F32), lo.astype(F32)).astype(BF)
    hi, lo = put(ecodet_ref[...], 0)
    ba_ref[...] = jnp.where(top, hi.astype(F32), lo.astype(F32)).astype(BF)
    hi, lo = put(xcode_ref[...], 4)
    xh_ref[...] = hi
    xl_ref[...] = lo
    mix = mix_ref[...]
    spread = spread_ref[...]
    same = same_ref[...].astype(F32)
    wide = nn(nn(spread, mix).astype(BF), spread.T)
    kl_ref[...] = (wide * same).astype(BF)
    wide = nn(spread, nt(mix.T, spread).astype(BF))
    klt_ref[...] = (wide * same).astype(BF)


def column_kernel(e_ref, perm_ref, lo_ref, hi_ref):
    half = lo_ref.shape[1]
    lanes = e_ref.shape[2]
    for m in range(0, e_ref.shape[0], 2):
        wide = jnp.concatenate([e_ref[m], e_ref[m + 1]], axis=1)
        picked = nn(perm_ref[...], wide).astype(BF)
        for i in range(2):
            lo_ref[m + i] = picked[:half, i * lanes : (i + 1) * lanes]
            hi_ref[m + i] = picked[half:, i * lanes : (i + 1) * lanes]


def edge_kernel(c_ref, e_ref, sel_ref, ce_ref, ee_ref):
    for m in range(c_ref.shape[0]):
        ce_ref[m] = nt(sel_ref[...], c_ref[m]).astype(BF)
        ee_ref[m] = nt(sel_ref[...], e_ref[m]).astype(BF)


def column_masks(cols, lanes, direction):
    row = lax.broadcasted_iota(jnp.int32, (1, cols, lanes), 1)
    wraps = []
    for offset in OFFSETS:
        o = direction * offset
        wraps.append((row >= cols - o) if o > 0 else (row < -o))
    return row, wraps


def forward_kernel(
    taps_ref, c_ref, e_ref, ch_ref, kl_ref, klt_ref, lf_ref, bf_ref, perm_ref, inc_ref, left_ref, right_ref
):
    rows = c_ref.shape[1]
    lanes = c_ref.shape[2]
    half = left_ref.shape[1]
    levels = half // 2
    cols = rows // levels

    @pl.when(pl.program_id(0) == 0)
    def _():
        inc_ref[...] = jnp.zeros_like(inc_ref)

    _, wraps = column_masks(cols, lanes, 1)
    inner = [jnp.where(w, 0.0, taps_ref[4 + t]) for t, w in enumerate(wraps)]
    outer = [jnp.where(w, taps_ref[4 + t], 0.0) for t, w in enumerate(wraps)]
    halo = nn(ch_ref[...], klt_ref[...])
    total = jnp.zeros((rows, lanes), F32)
    for pair in range(c_ref.shape[0] // 2):
        m0 = 2 * pair
        wide = jnp.concatenate([c_ref[m0], c_ref[m0 + 1]], axis=1)
        mixed = nn(kl_ref[...], wide).astype(BF)
        over = []
        for i in range(2):
            y = nn(mixed[:, i * lanes : (i + 1) * lanes], lf_ref[...])
            edge = tn(halo[8 * (m0 + i) : 8 * (m0 + i) + 8].astype(BF), bf_ref[...])
            row = (y[:, :lanes] + y[:, lanes:] + edge).reshape(levels, cols, lanes)
            loc = row
            out = jnp.zeros_like(row)
            for t in range(4):
                moved = pltpu.roll(row, (-OFFSETS[t]) % cols, 1)
                loc = loc + inner[t] * moved
                out = out + outer[t] * moved
            total = total + e_ref[m0 + i].astype(F32) * loc.reshape(rows, lanes)
            over.append(out.reshape(rows, lanes).astype(BF))
        picked = nn(perm_ref[...], jnp.concatenate(over, axis=1)).astype(BF)
        for i in range(2):
            right_ref[m0 + i] = picked[:half, i * lanes : (i + 1) * lanes]
            left_ref[m0 + i] = picked[half:, i * lanes : (i + 1) * lanes]
    inc_ref[...] += total


def obs_kernel(inc_ref, place_ref, q_ref, innov_ref, pulled_ref, edge_ref):
    rows, lanes = inc_ref.shape
    slots = place_ref.shape[1]
    place = place_ref[...]
    r = place // lanes
    c = place - r * lanes
    rt = (lax.broadcasted_iota(jnp.int32, (rows, slots), 0) == r).astype(F32).astype(BF)
    lane_ids = lax.broadcasted_iota(jnp.int32, (lanes, slots), 0)
    hit = lane_ids == c
    inc_t = inc_ref[...].T
    g = jnp.zeros((lanes, slots), F32)
    for part in part3(inc_t):
        g = g + nn(part, rt)
    at_slot = jnp.sum(jnp.where(hit, g, 0.0), axis=0, keepdims=True)
    misfit = q_ref[...] * (at_slot - innov_ref[...])
    e_ids = lax.broadcasted_iota(jnp.int32, (8, slots), 0)
    e_lane = jnp.where(e_ids < 2, e_ids, lanes - 4 + e_ids)
    e_hit = (e_lane == c) & (e_ids < 4)
    pulled = jnp.zeros((rows, lanes), F32)
    edge = jnp.zeros((8, rows), F32)
    for part in part3(misfit):
        part = part.astype(F32)
        pulled = pulled + nt(rt, jnp.where(hit, part, 0.0).astype(BF))
        edge = edge + nt(jnp.where(e_hit, part, 0.0).astype(BF), rt)
    pulled_ref[...] = pulled
    edge_ref[...] = edge


def adjoint_kernel(
    taps_ref, c_ref, e_ref, el_ref, er_ref, elat_ref, p_ref, pl_ref, pr_ref, plat_ref,
    xh_ref, xl_ref, la_ref, ba_ref, klt_ref, permt_ref, out_ref,
):
    rows = c_ref.shape[1]
    lanes = c_ref.shape[2]
    count = c_ref.shape[0]
    levels = el_ref.shape[1] // 2
    cols = rows // levels
    row_id = lax.broadcasted_iota(jnp.int32, (levels, cols, lanes), 1)
    plat = jnp.concatenate([plat_ref[...]] * count, axis=0)
    plane = (elat_ref[...].astype(F32) * plat).astype(BF)
    halo = nn(plane, xh_ref[...]) + nn(plane, xl_ref[...])
    for pair in range(count // 2):
        m0 = 2 * pair
        side = []
        for i in range(2):
            side.append(
                jnp.concatenate(
                    [
                        (er_ref[m0 + i].astype(F32) * pr_ref[...]).astype(BF),
                        (el_ref[m0 + i].astype(F32) * pl_ref[...]).astype(BF),
                    ],
                    axis=0,
                )
            )
        placed = nn(permt_ref[...], jnp.concatenate(side, axis=1))
        spread = []
        for i in range(2):
            own = (e_ref[m0 + i].astype(F32) * p_ref[...]).astype(BF).astype(F32)
            own = own.reshape(levels, cols, lanes)
            far = placed[:, i * lanes : (i + 1) * lanes].reshape(levels, cols, lanes)
            col = own
            for t in range(4):
                o = OFFSETS[t]
                from_far = (row_id >= cols - o) if o > 0 else (row_id < -o)
                col = col + taps_ref[4 + t] * pltpu.roll(jnp.where(from_far, far, own), o % cols, 1)
            y = nn(col.reshape(rows, lanes).astype(BF), la_ref[...])
            edge = tn(halo[8 * (m0 + i) : 8 * (m0 + i) + 8].astype(BF), ba_ref[...])
            spread.append((y[:, :lanes] + y[:, lanes:] + edge).astype(BF))
        back = nn(klt_ref[...], jnp.concatenate(spread, axis=1))
        for i in range(2):
            out_ref[m0 + i] = c_ref[m0 + i].astype(F32) + back[:, i * lanes : (i + 1) * lanes]


def full(shape):
    return pl.BlockSpec(shape, lambda g: (0,) * len(shape))


def shift(x, axis, step, wrap):
    n = lax.axis_size(axis)
    if step > 0:
        pairs = [(i, (i + 1) % n) for i in range(n if wrap else n - 1)]
    else:
        pairs = [((i + 1) % n, i) for i in range(n if wrap else n - 1)]
    return lax.ppermute(x, axis, pairs)


def butterfly(x, axis):
    n = lax.axis_size(axis)
    if n & (n - 1):
        return lax.psum(x, axis)
    bit = 1
    while bit < n:
        x = x + lax.ppermute(x, axis, [(i, i ^ bit) for i in range(n)])
        bit *= 2
    return x


def shards(
    control, ensemble, level_mix, lat_taps, lon_taps, obs_location, obs_count, obs_keep, innovation, obs_weight
):
    members, levels, cols, lanes = control.shape
    rows = levels * cols
    half = 2 * levels
    ext = rows + 2 * half
    block = 8 if members % 8 == 0 else 2
    steps = members // block
    c3 = control.reshape(members, rows, lanes)
    e3 = ensemble.reshape(members, rows, lanes)
    params = pltpu.CompilerParams(vmem_limit_bytes=VMEM_LIMIT)

    smem = pl.BlockSpec(memory_space=pltpu.SMEM)
    own = np.arange(rows)
    own_level, own_col = own // cols, own % cols
    h = np.arange(half)
    ext_level = np.concatenate([own_level, h // 2, h // 2])
    ext_col = np.concatenate([own_col, h % 2 - 2, cols + h % 2])
    same_level = ext_level[:, None] == own_level[None, :]
    xcode = np.where(same_level, code_of(own_col[None, :] - ext_col[:, None]), 0).astype(np.int32)
    lane_id = np.arange(lanes)
    lat_code = code_of(lane_id[:, None] - lane_id[None, :])
    edge_pos = np.array([-2, -1, lanes, lanes + 1] * 2)
    e_code = code_of(edge_pos[:, None] - lane_id[None, :])
    e_code_t = code_of(lane_id[None, :] - edge_pos[:, None])
    spread_levels = (own_level[:, None] == np.arange(levels)[None, :]).astype(np.float32)
    same_col = (own_col[:, None] == own_col[None, :]).astype(np.float32)
    sel_lane = np.array([0, 1, lanes - 2, lanes - 1, -1, -1, -1, -1])
    sel = jnp.asarray((sel_lane[:, None] == lane_id[None, :]).astype(np.float32).astype(BF))
    pick_level = np.concatenate([h // 2, h // 2])
    pick_col = np.concatenate([h % 2, cols - 2 + h % 2])
    perm_np = ((pick_level * cols + pick_col)[:, None] == own[None, :]).astype(np.float32)
    perm = jnp.asarray(perm_np.astype(BF))
    perm_t = jnp.asarray(perm_np.T.astype(BF))
    taps = jnp.concatenate([lat_taps, lon_taps])

    member_block = lambda a, b: pl.BlockSpec((block, a, b), lambda g: (g, 0, 0))
    low, high = pl.pallas_call(
        column_kernel,
        grid=(steps,),
        in_specs=[member_block(rows, lanes), full((2 * half, rows))],
        out_specs=[member_block(half, lanes)] * 2,
        out_shape=[jax.ShapeDtypeStruct((members, half, lanes), BF)] * 2,
        compiler_params=params,
        cost_estimate=pl.CostEstimate(flops=10**9, bytes_accessed=8 * 10**6, transcendentals=0),
    )(e3, perm)

    sel, e_left_src, e_right_src = lax.optimization_barrier((sel, high, low))
    e_left = shift(e_left_src, "lon", 1, True)
    e_right = shift(e_right_src, "lon", -1, True)
    ce, ee = pl.pallas_call(
        edge_kernel,
        grid=(steps,),
        in_specs=[member_block(rows, lanes)] * 2 + [full((8, lanes))],
        out_specs=[member_block(8, rows)] * 2,
        out_shape=[jax.ShapeDtypeStruct((members, 8, rows), BF)] * 2,
        compiler_params=params,
        cost_estimate=pl.CostEstimate(flops=10**9, bytes_accessed=11 * 10**6, transcendentals=0),
    )(c3, e3, sel)
    vm = pl.BlockSpec(memory_space=pltpu.VMEM)
    lf, la, bf, ba, lon_hi, lon_lo, kl, klt = pl.pallas_call(
        lambda *refs: setup_kernel(*refs[:8], *refs[9:], refs[8]),
        in_specs=[smem] + [vm] * 8,
        out_specs=[vm] * 8,
        out_shape=[jax.ShapeDtypeStruct(shape, BF) for shape in (
            (lanes, 2 * lanes), (lanes, 2 * lanes), (8, lanes), (8, lanes),
            (ext, rows), (ext, rows), (rows, rows), (rows, rows))],
        compiler_params=params,
        name="setup",
    )(taps, level_mix, jnp.asarray(lat_code), jnp.asarray(lat_code.T.copy()), jnp.asarray(e_code),
      jnp.asarray(e_code_t), jnp.asarray(spread_levels.astype(BF)), jnp.asarray(same_col.astype(BF)),
      jnp.asarray(xcode))

    both = jnp.concatenate([ce, ee], axis=0)
    before = shift(both[:, 2:4], "lat", 1, False)
    after = shift(both[:, 0:2], "lat", -1, False)
    lat_halo = jnp.concatenate([before, after], axis=1)
    lat_halo = jnp.concatenate([lat_halo, lat_halo], axis=1)
    ch, eh = lat_halo[:members], lat_halo[members:]
    corner = nt(eh.reshape(members * 8, rows), perm).astype(BF).reshape(members, 8, 2 * half)
    x_left = shift(corner[:, :4, half:], "lon", 1, True)
    x_right = shift(corner[:, :4, :half], "lon", -1, True)
    x_both = jnp.concatenate([x_left, x_right], axis=2)
    elat = jnp.concatenate([eh, jnp.concatenate([x_both, x_both], axis=1)], axis=2).reshape(members * 8, ext)

    inc, left, right = pl.pallas_call(
        forward_kernel,
        grid=(steps,),
        in_specs=[smem]
        + [member_block(rows, lanes)] * 2
        + [pl.BlockSpec((block * 8, rows), lambda g: (g, 0)), full((rows, rows)), full((rows, rows))]
        + [full((lanes, 2 * lanes)), full((8, lanes)), full((2 * half, rows))],
        out_specs=[full((rows, lanes))] + [member_block(half, lanes)] * 2,
        out_shape=[jax.ShapeDtypeStruct((rows, lanes), F32)]
        + [jax.ShapeDtypeStruct((members, half, lanes), BF)] * 2,
        compiler_params=params,
        cost_estimate=pl.CostEstimate(flops=10**10, bytes_accessed=20 * 10**6, transcendentals=0),
    )(taps, c3, e3, ch.reshape(members * 8, rows), kl, klt, lf, bf, perm)

    places = obs_location[0, 0]
    slots = places.shape[0]
    slot_ids = jnp.arange(slots, dtype=jnp.int32)
    live = (slot_ids < obs_count[0, 0]).astype(F32) * obs_keep[0, 0].astype(F32)
    q = live * obs_weight[0, 0]
    columns = ensemble.reshape(members, -1)[:, places]
    scaled = columns.astype(F32) * jnp.sqrt(q)[None, :]
    local_gram = jnp.dot(scaled, scaled.T, precision=lax.Precision.HIGHEST)
    total_obs = slots * lax.axis_size("lat") * lax.axis_size("lon")
    gram = butterfly(butterfly(local_gram, "lat"), "lon")
    upper = jnp.linalg.cholesky(jnp.eye(members, dtype=F32) + members / total_obs * gram).T

    to_left = jnp.sum(e_left.astype(F32) * left.astype(F32), axis=0)
    to_right = jnp.sum(e_right.astype(F32) * right.astype(F32), axis=0)
    from_right = shift(to_left, "lon", -1, True)
    from_left = shift(to_right, "lon", 1, True)
    cube = inc.reshape(levels, cols, lanes)
    zeros = jnp.zeros((levels, cols - 2, lanes), F32)
    cube = (
        cube
        + jnp.concatenate([from_left.reshape(levels, 2, lanes), zeros], axis=1)
        + jnp.concatenate([zeros, from_right.reshape(levels, 2, lanes)], axis=1)
    )

    pulled, p_edge = pl.pallas_call(
        obs_kernel,
        out_shape=[jax.ShapeDtypeStruct((rows, lanes), F32), jax.ShapeDtypeStruct((8, rows), F32)],
        compiler_params=params,
    )(cube.reshape(rows, lanes), places[None], q[None], innovation[0])

    p_before = shift(p_edge[2:4], "lat", 1, False)
    p_after = shift(p_edge[0:2], "lat", -1, False)
    plat = jnp.concatenate([p_before, p_after], axis=0)
    plat3 = plat.reshape(4, levels, cols)
    p3 = pulled.reshape(levels, cols, lanes)
    def packed(piece, corner):
        wide = jnp.pad(corner.reshape(4, half), ((0, 4), (0, lanes - half)))
        return jnp.concatenate([piece.reshape(half, lanes), wide], axis=0)

    p_left = shift(packed(p3[:, cols - 2 :], plat3[:, :, cols - 2 :]), "lon", 1, True)
    p_right = shift(packed(p3[:, :2], plat3[:, :, :2]), "lon", -1, True)
    px_left, px_right = p_left[half : half + 4, :half], p_right[half : half + 4, :half]
    p_left, p_right = p_left[:half], p_right[:half]
    plat = jnp.concatenate([plat, px_left, px_right], axis=1)
    plat = jnp.concatenate([plat, plat], axis=0)

    gradient = pl.pallas_call(
        adjoint_kernel,
        grid=(steps,),
        in_specs=[smem]
        + [member_block(rows, lanes)] * 2
        + [member_block(half, lanes)] * 2
        + [pl.BlockSpec((block * 8, ext), lambda g: (g, 0))]
        + [full((rows, lanes)), full((half, lanes)), full((half, lanes)), full((8, ext))]
        + [full((ext, rows))] * 2
        + [full((lanes, 2 * lanes)), full((8, lanes)), full((rows, rows)), full((rows, 2 * half))],
        out_specs=member_block(rows, lanes),
        out_shape=jax.ShapeDtypeStruct((members, rows, lanes), F32),
        compiler_params=params,
        cost_estimate=pl.CostEstimate(flops=10**10, bytes_accessed=24 * 10**6, transcendentals=0),
    )(taps, c3, e3, e_left, e_right, elat, pulled, p_left, p_right, plat,
      lon_hi, lon_lo, la, ba, klt, perm_t)
    return gradient.reshape(members, levels, cols, lanes), upper


def solution(mesh):
    in_specs = (
        P(None, None, "lon", "lat"),
        P(None, None, "lon", "lat"),
        P(),
        P(),
        P(),
        P("lon", "lat", None),
        P("lon", "lat"),
        P("lon", "lat", None),
        P("lon", "lat", None),
        P("lon", "lat", None),
    )
    out_specs = (P(None, None, "lon", "lat"), P())
    return jax.shard_map(shards, mesh=mesh, in_specs=in_specs, out_specs=out_specs, check_vma=False)
```

profile of v0, /device:TPU:1, one launch (start us, length us, event | category | flops | bytes accessed | tf_op | source)
XLA Modules:
  0.0 183.3 jit_solution(17678382549895658515)
XLA Ops:
  2.0 10.6 %copy.32 = bf16[80,32,8,128]{0,3,2,1:T(8,128)(2,1)} copy(bf16[80,32,8,128]{3,2,1,0:T(8,128)(2,1)} %param.21) | data formatting | bytes 10485760 | tf_op args[1]
  12.7 10.1 %gather_fusion = bf16[2048,80]{1,0:T(8,128)(2,1)S(1)} fusion(bf16[80,32768]{0,1:T(8,128)(2,1)} %bitcast.53, s32[2048]{0:T(1024)S(1)} %broadcast_clamp_fusion), kind=kCustom, calls=%fused_computation | custom fusion | bytes 663552 | tf_op jit(solution)/shard_map/gather | solution.py:340
  22.8 2.4 %fusion.1 = f32[80,80]{0,1:T(8,128)S(1)} fusion(bf16[2048,80]{1,0:T(8,128)(2,1)S(1)} %gather_fusion, f32[2048]{0:T(1024)S(1)} %multiply_sqrt_fusion), kind=kOutput, calls=%fused_computation.5 | convolution fusion | flops 157614080 | bytes 361472 | tf_op jit(solution)/shard_map/dot_general | solution.py:342
  25.2 8.2 %shard_map.203 = (bf16[80,64,128]{2,1,0:T(8,128)(2,1)}, bf16[80,64,128]{2,1,0:T(8,128)(2,1)}) custom-call(bf16[80,256,128]{2,1,0:T(8,128)(2,1)} %bitcast.49, bf16[128,256]{1,0:T(8,128)(2,1)} %constant.69.clone.perm_ref), custom_call_target="tpu_custom_call" | custom-call | flops 1000000000 | bytes 8000000 | tf_op jit(solution)/shard_map/pallas_call | solution.py:273
  33.4 9.6 %shard_map.204 = (bf16[80,8,256]{2,1,0:T(8,128)(2,1)}, bf16[80,8,256]{2,1,0:T(8,128)(2,1)}) custom-call(bf16[80,256,128]{2,1,0:T(8,128)(2,1)} %bitcast.54, bf16[80,256,128]{2,1,0:T(8,128)(2,1)} %bitcast.50, bf16[8,128]{1,0:T(8,128)(2,1)} %constant.68.clone.sel_ref), custom_call_target="tpu_custom_call" | custom-call | flops 1000000000 | bytes 11000000 | tf_op jit(solution)/shard_map/pallas_call | solution.py:286
  44.1 2.8 %collective-permute-start.13 = (f32[80,80]{0,1:T(8,128)S(1)}, f32[80,80]{0,1:T(8,128)S(1)}, u32[]{:S(2)}, u32[]{:S(2)}) collective-permute-start(f32[80,80]{0,1:T(8,128)S(1)} %add.58), channel_id=1, source_target_pairs={{0,16},{8,24},{16,0},{24,8},{1,17},{9,25},{17,1},{25,9},{2,18},{10... | collective-permute-start | bytes 76808 | tf_op jit(solution)/shard_map/ppermute | solution.py:230
  49.9 4.5 %collective-permute-start.2 = (bf16[160,2,256]{2,1,0:T(2,128)(2,1)S(1)}, bf16[160,2,256]{2,1,0:T(2,128)(2,1)S(1)}, u32[]{:S(2)}, u32[]{:S(2)}) collective-permute-start(bf16[160,2,256]{2,1,0:T(2,128)(2,1)S(1)} %get-tuple-element.44), channel_id=1, source_target_pairs={{0,8},{8,16},{16,24},{1,9},{9,17},{17,25},{2,10},{10,18},{18,26},{... | collective-permute-start | bytes 491528 | tf_op jit(solution)/shard_map/ppermute | solution.py:221
  54.4 1.9 %collective-permute-start.3 = (bf16[160,2,256]{2,1,0:T(2,128)(2,1)S(1)}, bf16[160,2,256]{2,1,0:T(2,128)(2,1)S(1)}, u32[]{:S(2)}, u32[]{:S(2)}) collective-permute-start(bf16[160,2,256]{2,1,0:T(2,128)(2,1)S(1)} %get-tuple-element.45), channel_id=1, source_target_pairs={{8,0},{16,8},{24,16},{9,1},{17,9},{25,17},{10,2},{18,10},{26,18},{... | collective-permute-start | bytes 491528 | tf_op jit(solution)/shard_map/ppermute | solution.py:221
  56.3 3.4 %collective-permute-start.1 = (bf16[80,64,128]{2,1,0:T(8,128)(2,1)}, bf16[80,64,128]{2,1,0:T(8,128)(2,1)S(1)}, u32[]{:S(2)}, u32[]{:S(2)}) collective-permute-start(bf16[80,64,128]{2,1,0:T(8,128)(2,1)} %get-tuple-element.25), channel_id=1, source_target_pairs={{1,0},{2,1},{3,2},{4,3},{5,4},{6,5},{7,6},{0,7},{9,8},{10,9},{11,1... | collective-permute-start | bytes 3932168 | tf_op jit(solution)/shard_map/ppermute | solution.py:221
  60.4 27.1 %collective-permute-done.15 = f32[80,80]{0,1:T(8,128)S(1)} collective-permute-done((f32[80,80]{0,1:T(8,128)S(1)}, f32[80,80]{0,1:T(8,128)S(1)}, u32[]{:S(2)}, u32[]{:S(2)}) %collective-permute-start.15) | collective-permute-done | bytes 25632 | tf_op jit(solution)/shard_map/ppermute | solution.py:230
  87.5 2.1 %collective-permute-start.16 = (f32[80,80]{0,1:T(8,128)S(1)}, f32[80,80]{0,1:T(8,128)S(1)}, u32[]{:S(2)}, u32[]{:S(2)}) collective-permute-start(f32[80,80]{0,1:T(8,128)S(1)} %add.61), channel_id=1, source_target_pairs={{0,4},{1,5},{2,6},{3,7},{4,0},{5,1},{6,2},{7,3},{8,12},{9,13},{10,... | collective-permute-start | bytes 76808 | tf_op jit(solution)/shard_map/ppermute | solution.py:230
  90.2 2.8 %setup.1 = (bf16[128,256]{1,0:T(8,128)(2,1)}, bf16[128,256]{1,0:T(8,128)(2,1)}, bf16[8,128]{1,0:T(8,128)(2,1)}, bf16[8,128]{1,0:T(8,128)(2,1)}, bf16[384,256]{1,...) custom-call(f32[8]{0:T(128)} %pad_maximum_fusion.2.refs_0_.taps_ref, ...), custom_call_target="tpu_custom_call" | custom-call | tf_op jit(solution)/shard_map/setup/pallas_call | solution.py:296
  93.1 7.3 %cholesky.20 = f32[80,80]{1,0:T(8,128)S(1)} custom-call(f32[80,80]{1,0:T(8,128)S(1)} %fusion.8), custom_call_target="Cholesky" | custom-call | tf_op jit(solution)/shard_map/jit(cholesky)/cholesky | solution.py:345
  104.3 21.6 %shard_map.205 = (f32[256,128]{1,0:T(8,128)}, bf16[80,64,128]{2,1,0:T(8,128)(2,1)}, bf16[80,64,128]{2,1,0:T(8,128)(2,1)}) custom-call(f32[8]{0:T(128)} %pad_maximum_fusion.2.refs_0_.taps_ref, bf16[80,256,128]{2,1,0:T(8,128)(2,1)} %bitcast.55, bf16[80,256,128]{2,1,0:T(8,128)(2,1)} %bitcast.51, bf16[640,256]{1,0:T(8,128)(2,1)} %get-tuple-element.42.ch_ref, ...), custom_call_target="tpu_custom_call" | custom-call | flops 10000000000 | bytes 20000000 | tf_op jit(solution)/shard_map/pallas_call | solution.py:321
  126.0 2.3 %multiply_reduce_fusion.1 = f32[64,128]{1,0:T(8,128)S(1)} fusion(bf16[80,64,128]{2,1,0:T(8,128)(2,1)} %get-tuple-element.34, bf16[80,64,128]{2,1,0:T(8,128)(2,1)S(1)} %collective-permute-done.1.er_ref), kind=kLoop, calls=%fused_computation.2 | loop fusion | flops 2613248 | bytes 2654208 | tf_op jit(solution)/shard_map/reduce_sum | solution.py:348
  128.3 4.1 %collective-permute-start.6 = (f32[64,128]{1,0:T(8,128)S(1)}, f32[64,128]{1,0:T(8,128)S(1)}, u32[]{:S(2)}, u32[]{:S(2)}) collective-permute-start(f32[64,128]{1,0:T(8,128)S(1)} %multiply_reduce_fusion.1), channel_id=1, source_target_pairs={{0,1},{1,2},{2,3},{3,4},{4,5},{5,6},{6,7},{7,0},{8,9},{9,10},{10,1... | collective-permute-start | bytes 98312 | tf_op jit(solution)/shard_map/ppermute | solution.py:221
  133.7 1.6 collective-permute-start.4
  135.3 2.8 %collective-permute-start.5 = (bf16[80,4,64]{2,1,0:T(4,128)(2,1)S(1)}, bf16[80,4,64]{2,1,0:T(4,128)(2,1)S(1)}, u32[]{:S(2)}, u32[]{:S(2)}) collective-permute-start(bf16[80,4,64]{2,1,0:T(4,128)(2,1)S(1)} %get-tuple-element.47), channel_id=1, source_target_pairs={{1,0},{2,1},{3,2},{4,3},{5,4},{6,5},{7,6},{0,7},{9,8},{10,9},{11,1... | collective-permute-start | bytes 122888 | tf_op jit(solution)/shard_map/ppermute | solution.py:221
  138.8 4.1 %shard_map.206 = (f32[256,128]{1,0:T(8,128)}, f32[8,256]{1,0:T(8,128)}) custom-call(f32[256,128]{1,0:T(8,128)} %fusion.7.inc_ref, s32[1,2048]{1,0:T(1,128)} %bitcast.64, f32[1,2048]{1,0:T(1,128)} %fusion.9.q_ref, f32[1,2048]{1,0:T(1,128)} %bitcast.68), custom_call_target="tpu_custom_call" | custom-call | tf_op jit(solution)/shard_map/pallas_call | solution.py:359
  143.7 5.2 %collective-permute-start.8 = (f32[2,256]{1,0:T(2,128)S(1)}, f32[2,256]{1,0:T(2,128)S(1)}, u32[]{:S(2)}, u32[]{:S(2)}) collective-permute-start(f32[2,256]{1,0:T(2,128)S(1)} %get-tuple-element.52), channel_id=1, source_target_pairs={{0,8},{8,16},{16,24},{1,9},{9,17},{17,25},{2,10},{10,18},{18,26},{... | collective-permute-start | bytes 6152 | tf_op jit(solution)/shard_map/ppermute | solution.py:221
  148.9 1.9 %collective-permute-start.9 = (f32[2,256]{1,0:T(2,128)S(1)}, f32[2,256]{1,0:T(2,128)S(1)}, u32[]{:S(2)}, u32[]{:S(2)}) collective-permute-start(f32[2,256]{1,0:T(2,128)S(1)} %get-tuple-element.53), channel_id=1, source_target_pairs={{8,0},{16,8},{24,16},{9,1},{17,9},{25,17},{10,2},{18,10},{26,18},{... | collective-permute-start | bytes 6152 | tf_op jit(solution)/shard_map/ppermute | solution.py:221
  151.9 2.0 %collective-permute-done.9 = f32[2,256]{1,0:T(2,128)S(1)} collective-permute-done((f32[2,256]{1,0:T(2,128)S(1)}, f32[2,256]{1,0:T(2,128)S(1)}, u32[]{:S(2)}, u32[]{:S(2)}) %collective-permute-start.9) | collective-permute-done | bytes 2080 | tf_op jit(solution)/shard_map/ppermute | solution.py:221
  158.0 3.7 %collective-permute-done.10 = f32[72,128]{1,0:T(8,128)S(1)} collective-permute-done((f32[72,128]{1,0:T(8,128)S(1)}, f32[72,128]{1,0:T(8,128)S(1)}, u32[]{:S(2)}, u32[]{:S(2)}) %collective-permute-start.10) | collective-permute-done | bytes 36896 | tf_op jit(solution)/shard_map/ppermute | solution.py:221
  163.0 20.3 %shard_map.207 = f32[80,256,128]{2,1,0:T(8,128)} custom-call(f32[8]{0:T(128)} %pad_maximum_fusion.2.refs_0_.taps_ref, bf16[80,256,128]{2,1,0:T(8,128)(2,1)} %bitcast.56, bf16[80,256,128]{2,1,0:T(8,128)(2,1)} %bitcast.52, bf16[80,64,128]{2,1,0:T(8,128)(2,1)} %copy-done.1, bf16[80,64,128]{2,1,0:T(8,128)(2,1)} %copy-done, ...), custom_call_target="tpu_custom_call" | custom-call | flops 10000000000 | bytes 24000000 | tf_op jit(solution)/shard_map/pallas_call | solution.py:381
  (84 shorter events, 19.4 us)
Async XLA Ops:
  2.0 10.6 %copy-start.7 = (s32[1,1,2048]{2,1,0:T(1,128)S(1)}, s32[1,1,2048]{2,1,0:T(1,128)}, u32[]{:S(2)}) copy-start(s32[1,1,2048]{2,1,0:T(1,128)} %param.25) | copy-start | bytes 24580
  12.6 10.1 %copy-start.5 = (f32[1,1,2048]{2,1,0:T(1,128)S(1)}, f32[1,1,2048]{2,1,0:T(1,128)}, u32[]{:S(2)}) copy-start(f32[1,1,2048]{2,1,0:T(1,128)} %param.29) | copy-start | bytes 24580
  25.1 18.9 %collective-permute-start.12 = (f32[80,80]{0,1:T(8,128)S(1)}, f32[80,80]{0,1:T(8,128)S(1)}, u32[]{:S(2)}, u32[]{:S(2)}) collective-permute-start(f32[80,80]{0,1:T(8,128)S(1)} %fusion.1), channel_id=1, source_target_pairs={{0,8},{8,0},{16,24},{24,16},{1,9},{9,1},{17,25},{25,17},{2,10},{10... | collective-permute-start | bytes 76808 | tf_op jit(solution)/shard_map/ppermute | solution.py:230
  43.0 16.8 %copy-start.6 = (s32[1,1,2048]{2,1,0:T(1,128)S(1)}, s32[1,1,2048]{2,1,0:T(1,128)}, u32[]{:S(2)}) copy-start(s32[1,1,2048]{2,1,0:T(1,128)} %param.27) | copy-start | bytes 24580
  43.0 46.6 %copy-start.8 = (f32[4]{0:T(128)S(1)}, f32[4]{0:T(128)}, u32[]{:S(2)}) copy-start(f32[4]{0:T(128)} %param.24) | copy-start | bytes 52
  43.0 46.6 %copy-start.9 = (f32[4]{0:T(128)S(1)}, f32[4]{0:T(128)}, u32[]{:S(2)}) copy-start(f32[4]{0:T(128)} %param.23) | copy-start | bytes 52
  44.1 4.7 %collective-permute-start.13 = (f32[80,80]{0,1:T(8,128)S(1)}, f32[80,80]{0,1:T(8,128)S(1)}, u32[]{:S(2)}, u32[]{:S(2)}) collective-permute-start(f32[80,80]{0,1:T(8,128)S(1)} %add.58), channel_id=1, source_target_pairs={{0,16},{8,24},{16,0},{24,8},{1,17},{9,25},{17,1},{25,9},{2,18},{10... | collective-permute-start | bytes 76808 | tf_op jit(solution)/shard_map/ppermute | solution.py:230
  48.8 10.9 %collective-permute-start.14 = (f32[80,80]{0,1:T(8,128)S(1)}, f32[80,80]{0,1:T(8,128)S(1)}, u32[]{:S(2)}, u32[]{:S(2)}) collective-permute-start(f32[80,80]{0,1:T(8,128)S(1)} %add.59), channel_id=1, source_target_pairs={{0,1},{1,0},{2,3},{3,2},{4,5},{5,4},{6,7},{7,6},{8,9},{9,8},{10,11... | collective-permute-start | bytes 76808 | tf_op jit(solution)/shard_map/ppermute | solution.py:230
  49.9 52.7 %collective-permute-start.2 = (bf16[160,2,256]{2,1,0:T(2,128)(2,1)S(1)}, bf16[160,2,256]{2,1,0:T(2,128)(2,1)S(1)}, u32[]{:S(2)}, u32[]{:S(2)}) collective-permute-start(bf16[160,2,256]{2,1,0:T(2,128)(2,1)S(1)} %get-tuple-element.44), channel_id=1, source_target_pairs={{0,8},{8,16},{16,24},{1,9},{9,17},{17,25},{2,10},{10,18},{18,26},{... | collective-permute-start | bytes 491528 | tf_op jit(solution)/shard_map/ppermute | solution.py:221
  54.4 48.2 %collective-permute-start.3 = (bf16[160,2,256]{2,1,0:T(2,128)(2,1)S(1)}, bf16[160,2,256]{2,1,0:T(2,128)(2,1)S(1)}, u32[]{:S(2)}, u32[]{:S(2)}) collective-permute-start(bf16[160,2,256]{2,1,0:T(2,128)(2,1)S(1)} %get-tuple-element.45), channel_id=1, source_target_pairs={{8,0},{16,8},{24,16},{9,1},{17,9},{25,17},{10,2},{18,10},{26,18},{... | collective-permute-start | bytes 491528 | tf_op jit(solution)/shard_map/ppermute | solution.py:221
  56.3 69.6 %collective-permute-start.1 = (bf16[80,64,128]{2,1,0:T(8,128)(2,1)}, bf16[80,64,128]{2,1,0:T(8,128)(2,1)S(1)}, u32[]{:S(2)}, u32[]{:S(2)}) collective-permute-start(bf16[80,64,128]{2,1,0:T(8,128)(2,1)} %get-tuple-element.25), channel_id=1, source_target_pairs={{1,0},{2,1},{3,2},{4,3},{5,4},{6,5},{7,6},{0,7},{9,8},{10,9},{11,1... | collective-permute-start | bytes 3932168 | tf_op jit(solution)/shard_map/ppermute | solution.py:221
  59.7 72.8 %collective-permute-start = (bf16[80,64,128]{2,1,0:T(8,128)(2,1)}, bf16[80,64,128]{2,1,0:T(8,128)(2,1)S(1)}, u32[]{:S(2)}, u32[]{:S(2)}) collective-permute-start(bf16[80,64,128]{2,1,0:T(8,128)(2,1)} %get-tuple-element.24), channel_id=1, source_target_pairs={{0,1},{1,2},{2,3},{3,4},{4,5},{5,6},{6,7},{7,0},{8,9},{9,10},{10,1... | collective-permute-start | bytes 3932168 | tf_op jit(solution)/shard_map/ppermute | solution.py:221
  59.7 27.8 %collective-permute-start.15 = (f32[80,80]{0,1:T(8,128)S(1)}, f32[80,80]{0,1:T(8,128)S(1)}, u32[]{:S(2)}, u32[]{:S(2)}) collective-permute-start(f32[80,80]{0,1:T(8,128)S(1)} %add.60), channel_id=1, source_target_pairs={{0,2},{1,3},{2,0},{3,1},{4,6},{5,7},{6,4},{7,5},{8,10},{9,11},{10,... | collective-permute-start | bytes 76808 | tf_op jit(solution)/shard_map/ppermute | solution.py:230
  87.5 5.5 %collective-permute-start.16 = (f32[80,80]{0,1:T(8,128)S(1)}, f32[80,80]{0,1:T(8,128)S(1)}, u32[]{:S(2)}, u32[]{:S(2)}) collective-permute-start(f32[80,80]{0,1:T(8,128)S(1)} %add.61), channel_id=1, source_target_pairs={{0,4},{1,5},{2,6},{3,7},{4,0},{5,1},{6,2},{7,3},{8,12},{9,13},{10,... | collective-permute-start | bytes 76808 | tf_op jit(solution)/shard_map/ppermute | solution.py:230
  93.1 11.0 %copy-start.3 = (bf16[128,256]{1,0:T(8,128)(2,1)S(1)}, bf16[128,256]{1,0:T(8,128)(2,1)}, u32[]{:S(2)}) copy-start(bf16[128,256]{1,0:T(8,128)(2,1)} %constant.69.clone.perm_ref) | copy-start | bytes 196612
  126.0 6.5 %copy-start.2 = (bf16[80,64,128]{2,1,0:T(8,128)(2,1)S(1)}, bf16[80,64,128]{2,1,0:T(8,128)(2,1)}, u32[]{:S(2)}) copy-start(bf16[80,64,128]{2,1,0:T(8,128)(2,1)} %get-tuple-element.35) | copy-start | bytes 3932164
  128.3 9.8 %collective-permute-start.6 = (f32[64,128]{1,0:T(8,128)S(1)}, f32[64,128]{1,0:T(8,128)S(1)}, u32[]{:S(2)}, u32[]{:S(2)}) collective-permute-start(f32[64,128]{1,0:T(8,128)S(1)} %multiply_reduce_fusion.1), channel_id=1, source_target_pairs={{0,1},{1,2},{2,3},{3,4},{4,5},{5,6},{6,7},{7,0},{8,9},{9,10},{10,1... | collective-permute-start | bytes 98312 | tf_op jit(solution)/shard_map/ppermute | solution.py:221
  133.5 4.6 %collective-permute-start.7 = (f32[64,128]{1,0:T(8,128)S(1)}, f32[64,128]{1,0:T(8,128)S(1)}, u32[]{:S(2)}, u32[]{:S(2)}) collective-permute-start(f32[64,128]{1,0:T(8,128)S(1)} %multiply_reduce_fusion), channel_id=1, source_target_pairs={{1,0},{2,1},{3,2},{4,3},{5,4},{6,5},{7,6},{0,7},{9,8},{10,9},{11,1... | collective-permute-start | bytes 98312 | tf_op jit(solution)/shard_map/ppermute | solution.py:221
  133.7 22.7 %collective-permute-start.4 = (bf16[80,4,64]{2,1,0:T(4,128)(2,1)S(1)}, bf16[80,4,64]{2,1,0:T(4,128)(2,1)S(1)}, u32[]{:S(2)}, u32[]{:S(2)}) collective-permute-start(bf16[80,4,64]{2,1,0:T(4,128)(2,1)S(1)} %get-tuple-element.46), channel_id=1, source_target_pairs={{0,1},{1,2},{2,3},{3,4},{4,5},{5,6},{6,7},{7,0},{8,9},{9,10},{10,1... | collective-permute-start | bytes 122888 | tf_op jit(solution)/shard_map/ppermute | solution.py:221
  135.3 21.0 %collective-permute-start.5 = (bf16[80,4,64]{2,1,0:T(4,128)(2,1)S(1)}, bf16[80,4,64]{2,1,0:T(4,128)(2,1)S(1)}, u32[]{:S(2)}, u32[]{:S(2)}) collective-permute-start(bf16[80,4,64]{2,1,0:T(4,128)(2,1)S(1)} %get-tuple-element.47), channel_id=1, source_target_pairs={{1,0},{2,1},{3,2},{4,3},{5,4},{6,5},{7,6},{0,7},{9,8},{10,9},{11,1... | collective-permute-start | bytes 122888 | tf_op jit(solution)/shard_map/ppermute | solution.py:221
  143.7 8.1 %collective-permute-start.8 = (f32[2,256]{1,0:T(2,128)S(1)}, f32[2,256]{1,0:T(2,128)S(1)}, u32[]{:S(2)}, u32[]{:S(2)}) collective-permute-start(f32[2,256]{1,0:T(2,128)S(1)} %get-tuple-element.52), channel_id=1, source_target_pairs={{0,8},{8,16},{16,24},{1,9},{9,17},{17,25},{2,10},{10,18},{18,26},{... | collective-permute-start | bytes 6152 | tf_op jit(solution)/shard_map/ppermute | solution.py:221
  148.9 4.9 %collective-permute-start.9 = (f32[2,256]{1,0:T(2,128)S(1)}, f32[2,256]{1,0:T(2,128)S(1)}, u32[]{:S(2)}, u32[]{:S(2)}) collective-permute-start(f32[2,256]{1,0:T(2,128)S(1)} %get-tuple-element.53), channel_id=1, source_target_pairs={{8,0},{16,8},{24,16},{9,1},{17,9},{25,17},{10,2},{18,10},{26,18},{... | collective-permute-start | bytes 6152 | tf_op jit(solution)/shard_map/ppermute | solution.py:221
  154.4 3.0 %collective-permute-start.11 = (f32[72,128]{1,0:T(8,128)S(1)}, f32[72,128]{1,0:T(8,128)S(1)}, u32[]{:S(2)}, u32[]{:S(2)}) collective-permute-start(f32[72,128]{1,0:T(8,128)S(1)} %select_maximum_fusion), channel_id=1, source_target_pairs={{1,0},{2,1},{3,2},{4,3},{5,4},{6,5},{7,6},{0,7},{9,8},{10,9},{11,1... | collective-permute-start | bytes 110600 | tf_op jit(solution)/shard_map/ppermute | solution.py:221
  156.2 5.6 %collective-permute-start.10 = (f32[72,128]{1,0:T(8,128)S(1)}, f32[72,128]{1,0:T(8,128)S(1)}, u32[]{:S(2)}, u32[]{:S(2)}) collective-permute-start(f32[72,128]{1,0:T(8,128)S(1)} %select_maximum_fusion.1), channel_id=1, source_target_pairs={{0,1},{1,2},{2,3},{3,4},{4,5},{5,6},{6,7},{7,0},{8,9},{9,10},{10,1... | collective-permute-start | bytes 110600 | tf_op jit(solution)/shard_map/ppermute | solution.py:221
  (3 other events, 9.1 us)
where the time goes:
time: 184 us; the launch traced here: 183 us
  Pallas kernels  66.6 us (36%)
  waiting for transfers between devices  33.7 us (18%)
  starting transfers between devices  33 us (18%)
  local copies, waits for them, and re-layouts  28.5 us (15%)
  other arithmetic  17.3 us (9%)
  matrix products  2.61 us (1%)
    ppermute x5, waiting for transfers between devices, butterfly(): x = x + lax.ppermute(x, axis, [(i, i ^ bit) for i in range(n)])  28 us
    ppermute x12, starting transfers between devices, shift(): return lax.ppermute(x, axis, pairs)  27.1 us
    pallas_call x1, Pallas kernels, shards(): pl.pallas_call(forward_kernel, grid=(steps,), in_specs=[smem] + [member_b...  21.6 us
    pallas_call x1, Pallas kernels, shards(): pl.pallas_call(adjoint_kernel, grid=(steps,), in_specs=[smem] + [member_b...  20.3 us
    unnamed x22, local copies, waits for them, and re-layouts  12.2 us
    gather x1, local copies, waits for them, and re-layouts, shards(): columns = ensemble.reshape(members, -1)[:, places]  10.1 us
    pallas_call x1, Pallas kernels, shards(): pl.pallas_call(edge_kernel, grid=(steps,), in_specs=[member_block(rows, l...  9.61 us
    pallas_call x1, Pallas kernels, shards(): pl.pallas_call(column_kernel, grid=(steps,), in_specs=[member_block(rows,...  8.18 us
  transfers between devices with their start and end apart: 17, of which 4 were waited for; matrix products, arithmetic and copies ran while one was open for 12% of the time, Pallas kernels for 25%

commit v1 on v0

v1 whole, which is shorter than its diff:
```python
import functools

import jax
import jax.numpy as jnp
from jax import lax
from jax.experimental import pallas as pl
from jax.experimental.pallas import tpu as pltpu
from jax.sharding import PartitionSpec as P

OFFSETS = (-2, -1, 1, 2)
F32, BF = jnp.float32, jnp.bfloat16
MIB = 1024 * 1024
MESH = pl.DeviceIdType.MESH


def nn(a, b):
    return jnp.dot(a, b, preferred_element_type=F32)


def nt(a, b):
    return lax.dot_general(a, b, (((1,), (1,)), ((), ())), preferred_element_type=F32)


def tn(a, b):
    return lax.dot_general(a, b, (((0,), (0,)), ((), ())), preferred_element_type=F32)


def split(x):
    hi = x.astype(BF)
    return hi, (x - hi.astype(F32)).astype(BF)


def iota(shape, axis):
    return lax.broadcasted_iota(jnp.int32, shape, axis)


def band(diff, taps_ref, base, sign):
    out = jnp.where(diff == 0, 1.0, 0.0)
    for t, offset in enumerate(OFFSETS):
        out = out + jnp.where(diff == sign * offset, taps_ref[base + t], 0.0)
    return out


def halo_place(h, levels, cols):
    side = h // (2 * levels)
    rest = h - side * 2 * levels
    d = rest // levels
    return rest - d * levels, d + side * (cols - 2), d - 2 + side * (cols + 2)


def setup_kernel(dims, taps_ref, count_ref, mix_ref, place_ref, keep_ref, weight_ref, innov_ref,
                 kf_ref, ka_ref, lf_ref, la_ref, q_ref, v_ref, meta_ref, start_ref):
    levels, cols, lanes = dims
    rows, half = levels * cols, 2 * levels
    ext = rows + 2 * half

    def ext_level_col(x):
        k, own, outer = halo_place(x - rows, levels, cols)
        inside = x < rows
        xk = x // cols
        return jnp.where(inside, xk, k), jnp.where(inside, x - xk * cols, own), jnp.where(
            inside, x - xk * cols, outer)

    mix = mix_ref[...]
    level, _, col = ext_level_col(iota((ext, rows), 0))
    y = iota((ext, rows), 1)
    taps = band((y - y // cols * cols) - col, taps_ref, 4, 1)
    pick = (ext_level_col(iota((ext, levels), 0))[0] == iota((ext, levels), 1)).astype(F32).astype(BF)
    put = (iota((levels, rows), 1) // cols == iota((levels, rows), 0)).astype(F32).astype(BF)
    hi, lo = split(nn(nn(pick, mix).astype(BF), put) * taps)
    kf_ref[0] = hi
    kf_ref[1] = lo
    level, _, col = ext_level_col(iota((rows, ext), 1))
    y = iota((rows, ext), 0)
    taps = band((y - y // cols * cols) - col, taps_ref, 4, 1)
    pick = (ext_level_col(iota((levels, ext), 1))[0] == iota((levels, ext), 0)).astype(F32).astype(BF)
    put = (iota((rows, levels), 0) // cols == iota((rows, levels), 1)).astype(F32).astype(BF)
    hi, lo = split(nn(put, nn(mix.T, pick).astype(BF)) * taps)
    ka_ref[0] = hi
    ka_ref[1] = lo
    diff = iota((lanes, lanes), 0) - iota((lanes, lanes), 1)
    lf_ref[...] = jnp.concatenate(split(band(diff, taps_ref, 0, 1)), axis=0)
    la_ref[...] = jnp.concatenate(split(band(diff, taps_ref, 0, -1)), axis=0)

    slots = place_ref.shape[1]
    chunk = 512 if slots % 512 == 0 else slots
    ids = iota((ext, chunk), 0)
    ids_level, ids_col, _ = ext_level_col(iota((ext, 1), 0))
    ids = jnp.broadcast_to(ids_level * cols + ids_col, (ext, chunk))
    lane_ids = iota((lanes, chunk), 0)
    total = jnp.zeros((ext, 4 * lanes), F32)
    for s in range(0, slots, chunk):
        place = place_ref[:, s : s + chunk]
        r = place // lanes
        c = place - r * lanes
        live = (iota((1, chunk), 1) + s < count_ref[0, 0]).astype(F32) * keep_ref[:, s : s + chunk].astype(F32)
        q = live * weight_ref[:, s : s + chunk]
        v = q * innov_ref[:, s : s + chunk]
        hit = lane_ids == c
        parts = []
        for x in (q, v):
            for part in split(x):
                parts.append(jnp.where(hit, part.astype(F32), 0.0).astype(BF))
        total = total + nt((ids == r).astype(F32).astype(BF), jnp.concatenate(parts, axis=0))
    q = total[:, :lanes] + total[:, lanes : 2 * lanes]
    v = total[:, 2 * lanes : 3 * lanes] + total[:, 3 * lanes :]
    q_ref[...] = q[:rows]
    v_ref[...] = v[:rows]
    held = q[rows:] > 0.0
    occupied = held.astype(F32).astype(BF)
    n = 2 * half
    before = (iota((lanes, lanes), 0) < iota((lanes, lanes), 1)).astype(F32).astype(BF)
    above = (iota((n, n), 1) < iota((n, n), 0)).astype(F32).astype(BF)
    within = nn(occupied, before)
    start = nn(above, nn(occupied, jnp.ones((lanes, lanes), BF)).astype(BF))
    rank = (start + within).astype(jnp.int32)
    last = max(slots // lanes - 1, 0)
    block = jnp.minimum(start.astype(jnp.int32) // lanes, last)
    relative = jnp.where(held, rank - block * lanes, -1)
    count = nt(jnp.ones((8, lanes), BF), occupied).astype(BF)
    below = (iota((n, n), 0) < iota((n, n), 1)).astype(F32).astype(BF)
    start_ref[...] = jnp.minimum(nn(count, below).astype(jnp.int32) // lanes, last)
    for side in range(2):
        at = slice(side * half, (side + 1) * half)
        meta_ref[side, 0] = relative[at].astype(F32)
        meta_ref[side, 1] = q[rows:][at]
        meta_ref[side, 2] = v[rows:][at]


def spot(relative_row, width):
    lanes = relative_row.shape[1]
    ranks = iota((width, lanes), 0).astype(F32)
    return jnp.where(jnp.broadcast_to(relative_row, (width, lanes)) == ranks, 1.0, 0.0).astype(BF)


def edge_rows(x_ref, lo_ref, hi_ref, members, lanes):
    group = 8
    out_row = iota((2 * 2 * group, lanes), 0)
    lane = iota((2 * 2 * group, lanes), 1)
    side = out_row // (2 * group)
    at = out_row - side * 2 * group
    want = at - at // 2 * 2 + side * (lanes - 2)

    def body(g, _):
        total = None
        for i in range(group):
            pick = jnp.where((lane == want) & (at // 2 == i), 1.0, 0.0).astype(BF)
            part = nt(pick, x_ref[g * group + i])
            total = part if total is None else total + part
        total = total.astype(BF)
        at_row = pl.multiple_of(g * 2 * group, 2 * group)
        lo_ref[pl.ds(at_row, 2 * group), :] = total[: 2 * group]
        hi_ref[pl.ds(at_row, 2 * group), :] = total[2 * group :]
        return 0

    lax.fori_loop(0, members // group, body, 0)


def gather_kernel(dims, start_ref, c_ref, e_ref, q_ref, meta_ref,
                  packed_ref, gram_ref, c_lo, c_hi, e_lo, e_hi, wide_ref, sum_ref):
    levels, cols, lanes = dims
    members = e_ref.shape[0]
    half = 2 * levels
    per = 2
    sum_ref[...] = jnp.zeros_like(sum_ref)

    def body(g, gram):
        base = pl.multiple_of(g * per * cols, per * cols)
        wide_ref[...] = e_ref[:, pl.ds(base, per * cols), :].astype(F32).reshape(members * per * cols, lanes)
        weight = q_ref[pl.ds(base, per * cols), :]
        for pair in range(0, per * cols, 2):
            plain, his, los = [], [], []
            for j in (pair, pair + 1):
                x = wide_ref[pl.ds(j, members, stride=per * cols), :]
                xb = x.astype(BF)
                plain.append(xb)
                hi, lo = split(x * weight[j : j + 1])
                his.append(hi)
                los.append(lo)
                col = j % cols
                low, high = col < 2, col >= cols - 2
                for side, here, d in ((0, low, col), (1, high, col - cols + 2)):
                    if not here:
                        continue
                    h = d * levels + g * per + j // cols
                    b = start_ref[0, side * half + h]
                    got = nt(xb, spot(meta_ref[side, 0, pl.ds(h, 1), :], 2 * lanes))
                    sum_ref[b] += got[:, :lanes]
                    sum_ref[b + 1] += got[:, lanes:]
            left = jnp.concatenate([jnp.concatenate(his, axis=1), jnp.concatenate(los, axis=1)], axis=0)
            gram = gram + nt(left, jnp.concatenate(plain, axis=1))
        return gram

    gram = lax.fori_loop(0, levels // per, body, jnp.zeros((2 * members, members), F32))
    gram_ref[...] = gram[:members] + gram[members:]
    blocks = packed_ref.shape[0]
    for b in range(blocks):
        packed_ref[b] = sum_ref[b].astype(BF)
    edge_rows(c_ref, c_lo, c_hi, members, lanes)
    edge_rows(e_ref, e_lo, e_hi, members, lanes)


def exchange_kernel(dims, sizes, taps_ref, c_ref, e_ref, q_ref, v_ref, kf_ref, lf_ref, packed_ref, meta_ref,
                    start_ref, gram_ref, c_lo, c_hi, e_lo, e_hi,
                    p_ref, px_ref, ext_ref, edge_b_ref, edge_a_ref, total_ref,
                    got_ref, got_meta, got_start, start_smem, lat_c, lat_e, lat_x, own_x, outer_ref, inc_ref,
                    wide_ref, send_inc, got_inc, p_edge, got_edge, gram_in,
                    far_sem, far_recv, lat_sem, lat_recv, x_sem, x_recv, inc_sem, inc_recv,
                    pe_sem, pe_recv, gram_sem, gram_recv, smem_sem):
    levels, cols, lanes = dims
    n_lat, n_lon = sizes
    members, rows = c_ref.shape[0], c_ref.shape[1]
    half = 2 * levels
    ext = rows + 2 * half
    lat, lon = lax.axis_index("lat"), lax.axis_index("lon")
    left, right = lax.rem(lon + n_lon - 1, n_lon), lax.rem(lon + 1, n_lon)
    has_before, has_after = lat > 0, lat < n_lat - 1

    def flip(x, bit):
        return x + bit - 2 * bit * (x // bit - x // (2 * bit) * 2)

    partners = [("lat", 1 << i) for i in range(n_lat.bit_length() - 1)]
    partners += [("lon", 1 << i) for i in range(n_lon.bit_length() - 1)]
    barrier = pltpu.get_barrier_semaphore()

    def greet(where):
        pl.semaphore_signal(barrier, inc=1, device_id=where, device_id_type=MESH)

    greet({"lon": left})
    greet({"lon": right})

    @pl.when(has_before)
    def _():
        greet({"lat": lat - 1})

    @pl.when(has_after)
    def _():
        greet({"lat": lat + 1})

    for axis, bit in partners:
        greet({axis: flip(lat if axis == "lat" else lon, bit)})
    pl.semaphore_wait(barrier, 2 + len(partners) + has_before.astype(jnp.int32) + has_after.astype(jnp.int32))

    def remote(src, dst, s, r, where):
        return pltpu.make_async_remote_copy(
            src_ref=src, dst_ref=dst, send_sem=s, recv_sem=r, device_id=where, device_id_type=MESH)

    blocks = packed_ref.shape[0]
    far = []
    for slot, to in ((0, right), (1, left)):
        mine = 1 - slot
        far.append(remote(meta_ref.at[mine], got_meta.at[slot], far_sem.at[slot, 0], far_recv.at[slot, 0], {"lon": to}))
        far.append(remote(start_ref, got_start.at[slot], far_sem.at[slot, 1], far_recv.at[slot, 1], {"lon": to}))
    for slot, to in ((0, right), (1, left)):
        far.append(remote(packed_ref, got_ref.at[slot, pl.ds(0, blocks)], far_sem.at[slot, 2], far_recv.at[slot, 2],
                          {"lon": to}))

    def lat_pairs(lo, hi, dst, s, r, k):
        up = remote(hi, dst.at[0], s.at[0, k], r.at[0, k], {"lat": lat + 1})
        down = remote(lo, dst.at[1], s.at[1, k], r.at[1, k], {"lat": lat - 1})
        return up, down

    def lat_start(pairs):
        for up, down in pairs:
            pl.when(has_after)(up.start)
            pl.when(has_before)(down.start)

    def lat_wait(pairs):
        for up, down in pairs:
            pl.when(has_after)(up.wait_send)
            pl.when(has_before)(down.wait_send)
            pl.when(has_before)(up.wait_recv)
            pl.when(has_after)(down.wait_recv)

    near = [lat_pairs(c_lo, c_hi, lat_c, lat_sem, lat_recv, 0), lat_pairs(e_lo, e_hi, lat_e, lat_sem, lat_recv, 1)]
    lat_start(near)
    for copy in far:
        copy.start()

    @pl.when(jnp.logical_not(has_before))
    def _():
        lat_c[0] = jnp.zeros_like(lat_c[0])
        lat_e[0] = jnp.zeros_like(lat_e[0])
        lat_x[0] = jnp.zeros_like(lat_x[0])
        got_edge[0] = jnp.zeros_like(got_edge[0])

    @pl.when(jnp.logical_not(has_after))
    def _():
        lat_c[1] = jnp.zeros_like(lat_c[1])
        lat_e[1] = jnp.zeros_like(lat_e[1])
        lat_x[1] = jnp.zeros_like(lat_x[1])
        got_edge[1] = jnp.zeros_like(got_edge[1])

    for slot in range(2):
        got_ref[slot, blocks] = jnp.zeros_like(got_ref[slot, blocks])
    inc_ref[...] = jnp.zeros_like(inc_ref)
    total_ref[...] = gram_ref[...]

    def forward(pair, _):
        smooth = []
        for i in range(2):
            x = c_ref[2 * pair + i]
            smooth.append(nn(jnp.concatenate([x, x], axis=1), lf_ref[...]).astype(BF))
        y = jnp.concatenate(smooth, axis=1)
        out = nn(kf_ref[0], y) + nn(kf_ref[1], y)
        total = inc_ref[...]
        for i in range(2):
            m = 2 * pair + i
            part = out[:, i * lanes : (i + 1) * lanes]
            total = total + e_ref[m].astype(F32) * part[:rows]
            outer_ref[m] = part[rows:].astype(BF)
        inc_ref[...] = total
        return 0

    pairs = members // 2
    steps = len(partners) + 1
    cuts = [pairs * i // steps for i in range(steps + 1)]
    for i in range(steps):
        copy = None
        if i < len(partners):
            axis, bit = partners[i]
            gram_in[i, 0] = total_ref[...]
            copy = remote(gram_in.at[i, 0], gram_in.at[i, 1], gram_sem.at[i], gram_recv.at[i],
                          {axis: flip(lat if axis == "lat" else lon, bit)})
            copy.start()
        lax.fori_loop(cuts[i], cuts[i + 1], forward, 0)
        if copy is not None:
            copy.wait()
            total_ref[...] = total_ref[...] + gram_in[i, 1]

    lat_wait(near)
    odd = iota((2 * members, ext), 0) % 2
    mixed = []
    for side in range(2):
        mixed.append(nt(lat_c[side], kf_ref[0]) + nt(lat_c[side], kf_ref[1]))
    edge = [
        taps_ref[0] * mixed[0] + jnp.where(odd == 0, taps_ref[1], 0.0) * pltpu.roll(mixed[0], 2 * members - 1, 0),
        taps_ref[3] * mixed[1] + jnp.where(odd == 1, taps_ref[2], 0.0) * pltpu.roll(mixed[1], 1, 0),
    ]
    edge_lane = iota((8, lanes), 1)
    edge_row = iota((8, lanes), 0)

    def place(e_rows, values):
        out = None
        for side in range(2):
            x = e_rows[side].astype(F32) * values[side]
            x = x.reshape(members // 4, 8, x.shape[1]).sum(axis=0)
            first = side * (lanes - 2)
            pick = jnp.where(edge_lane == first + edge_row % 2, 1.0, 0.0).astype(BF)
            hi, lo = split(x)
            part = tn(hi, pick) + tn(lo, pick)
            out = part if out is None else out + part
        return out

    inc_ref[...] += place((e_lo[...], e_hi[...]), [x[:, :rows] for x in edge])
    edge = [x[:, rows:] for x in edge]

    for copy in far:
        copy.wait()
    for slot in range(2):
        copy = pltpu.make_async_copy(got_start.at[slot], start_smem.at[slot], smem_sem)
        copy.start()
        copy.wait()
    for slot in range(2):
        def expand(h, _, slot=slot):
            b = start_smem[slot, 0, (1 - slot) * half + h]
            hot = spot(got_meta[slot, 0, pl.ds(h, 1), :], 2 * lanes)
            got = nn(jnp.concatenate([got_ref[slot, b], got_ref[slot, b + 1]], axis=1), hot)
            wide_ref[pl.ds(slot * half + h, members, stride=2 * half), :] = got
            return 0

        lax.fori_loop(0, half, expand, 0)

    def outer(m, total):
        at = pl.multiple_of(m * 2 * half, 2 * half)
        x = wide_ref[pl.ds(at, 2 * half), :]
        ext_ref[m] = x.astype(BF)
        return total + x * outer_ref[m].astype(F32)

    given = lax.fori_loop(0, members, outer, jnp.zeros((2 * half, lanes), F32))
    edge_rows(ext_ref, own_x.at[0], own_x.at[1], members, lanes)
    across = [lat_pairs(own_x.at[0], own_x.at[1], lat_x, x_sem, x_recv, 0)]
    lat_start(across)
    given = given + place((own_x[0], own_x[1]), edge)

    for d in range(2):
        at = slice(d * levels, (d + 1) * levels)
        send_inc[0, 0, at] = inc_ref[pl.ds(cols - 2 + d, levels, stride=cols), :]
        send_inc[1, 0, at] = inc_ref[pl.ds(d, levels, stride=cols), :]
    send_inc[0, 1] = given[half:]
    send_inc[1, 1] = given[:half]
    swap = []
    for slot, to in ((0, right), (1, left)):
        swap.append(remote(send_inc.at[slot], got_inc.at[slot], inc_sem.at[slot], inc_recv.at[slot], {"lon": to}))
    for copy in swap:
        copy.start()
    for copy in swap:
        copy.wait()
    for slot in range(2):
        px_ref[slot * half : (slot + 1) * half] = (
            got_meta[slot, 1] * (got_inc[slot, 0] + given[slot * half : (slot + 1) * half]) - got_meta[slot, 2])
        for d in range(2):
            at = pl.ds(slot * (cols - 2) + d, levels, stride=cols)
            inc_ref[at, :] = inc_ref[at, :] + got_inc[slot, 1, d * levels : (d + 1) * levels]
    p_ref[...] = q_ref[...] * inc_ref[...] - v_ref[...]

    want = edge_row % 2 + jnp.where(edge_row < 2, 0, lanes - 2)
    pick = jnp.where((edge_lane == want) & (edge_row < 4), 1.0, 0.0).astype(BF)
    for ref, at in ((p_ref, slice(0, rows)), (px_ref, slice(rows, ext))):
        hi, lo = split(ref[...])
        p_edge[:, at] = nt(pick, hi) + nt(pick, lo)
    last = [lat_pairs(p_edge, p_edge, got_edge, pe_sem, pe_recv, 0)]
    lat_start(last)
    lat_wait(across)
    lat_wait(last)
    for side, out_ref in ((0, edge_b_ref), (1, edge_a_ref)):
        first = 2 - 2 * side
        got = got_edge[side]
        p = jnp.where(odd == 0, got[first : first + 1], got[first + 1 : first + 2])
        e = jnp.concatenate([lat_e[side], lat_x[side]], axis=1)
        out_ref[...] = (e.astype(F32) * p).astype(BF)


def adjoint_kernel(dims, block, taps_ref, c_ref, e_ref, ext_ref, p_ref, px_ref, edge_b_ref, edge_a_ref, ka_ref,
                   la_ref, out_ref, edge_ref):
    levels, cols, lanes = dims
    members, rows = c_ref.shape[0], c_ref.shape[1]
    step = pl.program_id(0)
    per = lanes // 4

    @pl.when(step == 0)
    def _():
        groups = edge_ref.shape[0]
        shape = (2 * members, groups * lanes)
        src, dst = iota(shape, 0), iota(shape, 1)
        same = src // 2 == dst // 4
        u, t = src % 2, dst % 4
        total = jnp.zeros((rows, groups * lanes), F32)
        for side, ref in ((0, edge_b_ref), (1, edge_a_ref)):
            z = (nt(ka_ref[0], ref[...]) + nt(ka_ref[1], ref[...])).astype(BF)
            if side == 0:
                w = jnp.where(t == u + 2, taps_ref[3], 0.0) + jnp.where((t == 2) & (u == 1), taps_ref[2], 0.0)
            else:
                w = jnp.where(t == u, taps_ref[0], 0.0) + jnp.where((t == 1) & (u == 0), taps_ref[1], 0.0)
            for part in split(jnp.where(same, w, 0.0)):
                total = total + nn(z, part)
        for g in range(groups):
            edge_ref[g] = total[:, g * lanes : (g + 1) * lanes]

    lane = iota((rows, lanes), 1)
    at_edge = (lane < 2) | (lane >= lanes - 2)
    p, px = p_ref[...], px_ref[...]

    for pair in range(block // 2):
        wide = []
        for i in range(2):
            m = step * block + 2 * pair + i
            own = (e_ref[m].astype(F32) * p).astype(BF)
            far = (ext_ref[m].astype(F32) * px).astype(BF)
            wide.append(jnp.concatenate([own, far], axis=0))
        wide = jnp.concatenate(wide, axis=1)
        z = (nn(ka_ref[0], wide) + nn(ka_ref[1], wide)).astype(BF)
        for i in range(2):
            m = step * block + 2 * pair + i
            zi = z[:, i * lanes : (i + 1) * lanes]
            y = nn(jnp.concatenate([zi, zi], axis=1), la_ref[...])
            g = m // per
            turned = pltpu.roll(edge_ref[g], lax.rem(2 * lanes - 2 - 4 * (m - g * per), lanes), 1)
            out_ref[2 * pair + i] = c_ref[m].astype(F32) + y + jnp.where(at_edge, turned, 0.0)


def shards(
    control, ensemble, level_mix, lat_taps, lon_taps, obs_location, obs_count, obs_keep, innovation, obs_weight
):
    members, levels, cols, lanes = control.shape
    dims = (levels, cols, lanes)
    rows, half = levels * cols, 2 * levels
    ext = rows + 2 * half
    slots = obs_location.shape[2]
    blocks = slots // lanes
    n_lat, n_lon = lax.axis_size("lat"), lax.axis_size("lon")
    vm, sm = pl.BlockSpec(memory_space=pltpu.VMEM), pl.BlockSpec(memory_space=pltpu.SMEM)
    here = functools.partial(pltpu.with_memory_space_constraint, memory_space=pltpu.VMEM)
    e3 = here(ensemble.reshape(members, rows, lanes))
    c3 = here(control.reshape(members, rows, lanes))
    taps = jnp.concatenate([lat_taps, lon_taps])

    def sds(shape, dtype=F32):
        return jax.ShapeDtypeStruct(shape, dtype)

    kf, ka, lf, la, q, v, meta, start = pl.pallas_call(
        functools.partial(setup_kernel, dims),
        in_specs=[sm, sm] + [vm] * 5,
        out_specs=[vm] * 8,
        out_shape=[sds((2, ext, rows), BF), sds((2, rows, ext), BF), sds((2 * lanes, lanes), BF),
                   sds((2 * lanes, lanes), BF), sds((rows, lanes)), sds((rows, lanes)),
                   sds((2, 3, half, lanes)), sds((8, 2 * half), jnp.int32)],
        compiler_params=pltpu.CompilerParams(vmem_limit_bytes=8 * MIB),
        name="setup",
    )(taps, obs_count, level_mix, obs_location[0], obs_keep[0], obs_weight[0], innovation[0])

    edges = [sds((2 * members, rows), BF)] * 4
    packed, gram, c_lo, c_hi, e_lo, e_hi = pl.pallas_call(
        functools.partial(gather_kernel, dims),
        in_specs=[sm] + [vm] * 4,
        out_specs=[vm] * 6,
        out_shape=[sds((blocks, members, lanes), BF), sds((members, members))] + edges,
        scratch_shapes=[pltpu.VMEM((members * 2 * cols, lanes), F32),
                        pltpu.VMEM((blocks + 1, members, lanes), F32)],
        compiler_params=pltpu.CompilerParams(vmem_limit_bytes=12 * MIB),
        name="gather",
    )(start, c3, e3, q, meta)

    n_bits = (n_lat.bit_length() - 1) + (n_lon.bit_length() - 1)
    dma = pltpu.SemaphoreType.DMA
    p, px, e_ext, edge_b, edge_a, gram = pl.pallas_call(
        functools.partial(exchange_kernel, dims, (n_lat, n_lon)),
        in_specs=[sm] + [vm] * 14,
        out_specs=[vm] * 6,
        out_shape=[sds((rows, lanes)), sds((2 * half, lanes)), sds((members, 2 * half, lanes), BF),
                   sds((2 * members, ext), BF), sds((2 * members, ext), BF), sds((members, members))],
        scratch_shapes=[
            pltpu.VMEM((2, blocks + 1, members, lanes), BF),
            pltpu.VMEM((2, 3, half, lanes), F32),
            pltpu.VMEM((2, 8, 2 * half), jnp.int32),
            pltpu.SMEM((2, 8, 2 * half), jnp.int32),
            pltpu.VMEM((2, 2 * members, rows), BF),
            pltpu.VMEM((2, 2 * members, rows), BF),
            pltpu.VMEM((2, 2 * members, 2 * half), BF),
            pltpu.VMEM((2, 2 * members, 2 * half), BF),
            pltpu.VMEM((members, 2 * half, lanes), BF),
            pltpu.VMEM((rows, lanes), F32),
            pltpu.VMEM((members * 2 * half, lanes), F32),
            pltpu.VMEM((2, 2, half, lanes), F32),
            pltpu.VMEM((2, 2, half, lanes), F32),
            pltpu.VMEM((8, ext), F32),
            pltpu.VMEM((2, 8, ext), F32),
            pltpu.VMEM((n_bits, 2, members, members), F32),
            dma((2, 3)), dma((2, 3)), dma((2, 2)), dma((2, 2)), dma((2, 1)), dma((2, 1)), dma((2,)), dma((2,)),
            dma((2, 1)), dma((2, 1)), dma((n_bits,)), dma((n_bits,)), dma,
        ],
        compiler_params=pltpu.CompilerParams(
            vmem_limit_bytes=14 * MIB, collective_id=0, has_side_effects=True),
        name="exchange",
    )(taps, c3, e3, q, v, kf, lf, packed, meta, start, gram, c_lo, c_hi, e_lo, e_hi)

    block = 8 if members % 8 == 0 else 2
    groups = -(-4 * members // lanes)
    gradient = pl.pallas_call(
        functools.partial(adjoint_kernel, dims, block),
        grid=(members // block,),
        in_specs=[sm] + [vm] * 9,
        out_specs=pl.BlockSpec((block, rows, lanes), lambda g: (g, 0, 0)),
        out_shape=sds((members, rows, lanes)),
        scratch_shapes=[pltpu.VMEM((groups, rows, lanes), F32)],
        compiler_params=pltpu.CompilerParams(vmem_limit_bytes=8 * MIB),
        name="adjoint",
    )(taps, c3, e3, e_ext, p, px, edge_b, edge_a, ka, la)
    total_obs = slots * n_lat * n_lon
    upper = jnp.linalg.cholesky(jnp.eye(members, dtype=F32) + members / total_obs * gram).T
    return gradient.reshape(members, levels, cols, lanes), upper


def solution(mesh):
    in_specs = (
        P(None, None, "lon", "lat"),
        P(None, None, "lon", "lat"),
        P(),
        P(),
        P(),
        P("lon", "lat", None),
        P("lon", "lat"),
        P("lon", "lat", None),
        P("lon", "lat", None),
        P("lon", "lat", None),
    )
    out_specs = (P(None, None, "lon", "lat"), P())
    return jax.shard_map(shards, mesh=mesh, in_specs=in_specs, out_specs=out_specs, check_vma=False)
```

time: 184 us -> 150 us (0.82)
  Pallas kernels: 66.6 us -> 113 us
  waiting for transfers between devices: 33.7 us -> 0 us
  starting transfers between devices: 33 us -> 0 us
  local copies, waits for them, and re-layouts: 28.5 us -> 18.5 us
  matrix products: 2.61 us -> 0 us
    pallas_call x6 -> x4, Pallas kernels: 66.6 us -> 113 us  [the longest x1 72.9 us: shards(): pl.pallas_call(functools.partial(exchange_kernel, dims, (n_lat, n_lon)),...]
    ppermute x17 -> x0, waiting for transfers between devices: 33.7 us -> none  [the longest x5 28 us: butterfly(): x = x + lax.ppermute(x, axis, [(i, i ^ bit) for i in range(n)])]
    ppermute x17 -> x0, starting transfers between devices: 33 us -> none  [the longest x12 27.1 us: shift(): return lax.ppermute(x, axis, pairs)]
    gather x1 -> x0, local copies, waits for them, and re-layouts: 10.1 us -> none  [shards(): columns = ensemble.reshape(members, -1)[:, places]]
    slice x11 -> x0, local copies, waits for them, and re-layouts: 4.06 us -> none  [the longest x3 1.4 us: shards(): p_right = shift(packed(p3[:, :2], plat3[:, :, :2]), 'lon', -1, True)]
    reduce_sum x2 -> x0, other arithmetic: 2.86 us -> none  [the longest x1 2.32 us: shards(): to_right = jnp.sum(e_right.astype(F32) * right.astype(F32), axis=0)]
    dot_general x2 -> x0, matrix products: 2.61 us -> none  [the longest x1 2.38 us: shards(): local_gram = jnp.dot(scaled, scaled.T, precision=lax.Precision.HIGHEST)]
    another operation x3, other arithmetic: 8.13 us -> 10.3 us  [shards(): jnp.linalg.cholesky(jnp.eye(members, dtype=F32) + members / total_obs * g...]
  transfers between devices with their start and end apart: 17 -> 0, of which waited for: 4 -> 0; matrix products, arithmetic and copies ran while one was open for 12% -> 0% of each run, Pallas kernels for 25% -> 0%
where the time goes in v1:
time: 150 us; the launch traced here: 149 us
  Pallas kernels  113 us (75%)
  local copies, waits for them, and re-layouts  18.5 us (12%)
  other arithmetic  16 us (11%)
    pallas_call x1, Pallas kernels, shards(): pl.pallas_call(functools.partial(exchange_kernel, dims, (n_lat, n_lon)),...  72.9 us
    pallas_call x1, Pallas kernels, shards(): pl.pallas_call(functools.partial(adjoint_kernel, dims, block), grid=(memb...  21.1 us
    pallas_call x1, Pallas kernels, shards(): pl.pallas_call(functools.partial(gather_kernel, dims), in_specs=[sm] + [v...  16.5 us
    unnamed x22, local copies, waits for them, and re-layouts  14.1 us
    another operation x3, other arithmetic, shards(): jnp.linalg.cholesky(jnp.eye(members, dtype=F32) + members / total_obs * g...  10.3 us

profile of v1, /device:TPU:1, one launch (start us, length us, event | category | flops | bytes accessed | tf_op | source)
XLA Modules:
  0.0 148.7 jit_solution(13049012500480605190)
XLA Ops:
  1.3 0.7 pad_maximum_fusion.taps_ref
  2.0 0.7 copy-done.6
  2.7 0.7 copy-done.7
  3.4 0.7 copy-done.8
  4.1 0.7 copy-done.9
  4.8 0.7 copy-done.10
  5.5 2.4 %setup.1 = (bf16[2,384,256]{2,1,0:T(8,128)(2,1)S(1)}, bf16[2,256,384]{2,1,0:T(8,128)(2,1)S(1)}, bf16[256,128]{1,0:T(8,128)(2,1)S(1)}, bf16[256,128]{1,0:T(8,128)...) custom-call(f32[8]{0:T(128)S(1)} %pad_maximum_fusion.taps_ref, ...), custom_call_target="tpu_custom_call" | custom-call | tf_op jit(solution)/shard_map/setup/pallas_call | solution.py:491
  8.0 2.5 %copy-done = bf16[80,32,8,128]{3,2,1,0:T(8,128)(2,1)S(1)} copy-done((bf16[80,32,8,128]{3,2,1,0:T(8,128)(2,1)S(1)}, bf16[80,32,8,128]{3,2,1,0:T(8,128)(2,1)}, u32[]{:S(2)}) %copy-start) | copy-done | bytes 5242904
  10.4 2.5 %copy-done.3 = bf16[80,32,8,128]{3,2,1,0:T(8,128)(2,1)S(1)} copy-done((bf16[80,32,8,128]{3,2,1,0:T(8,128)(2,1)S(1)}, bf16[80,32,8,128]{3,2,1,0:T(8,128)(2,1)}, u32[]{:S(2)}) %copy-start.3) | copy-done | bytes 5242904
  12.9 16.5 %gather.1 = (bf16[16,80,128]{2,1,0:T(8,128)(2,1)S(1)}, f32[80,80]{1,0:T(8,128)S(1)}, bf16[160,256]{1,0:T(8,128)(2,1)S(1)}, bf16[160,256]{1,0:T(8,128)(2,1)S(1)},...) custom-call(s32[8,128]{1,0:T(8,128)S(1)} %get-tuple-element.26.start_ref, bf16[80,256,128]{2,1,0:T(8,128)(2,1)S(1)} %bitcast.13, ...), custom_call_target="tpu_custom_call" | custom-call | tf_op jit(solution)/shard_map/gather/pallas_call | solution.py:503
  29.4 72.9 %exchange.1 = (f32[256,128]{1,0:T(8,128)S(1)}, f32[128,128]{1,0:T(8,128)S(1)}, bf16[80,128,128]{2,1,0:T(8,128)(2,1)S(1)}, bf16[160,384]{1,0:T(8,128)(2,1)S(1)}, ...) custom-call(f32[8]{0:T(128)S(1)} %pad_maximum_fusion.taps_ref, bf16[80,256,128]{2,1,0:T(8,128)(2,1)S(1)} %bitcast.14, ...), custom_call_target="tpu_custom_call" | custom-call | tf_op jit(solution)/shard_map/exchange/pallas_call | solution.py:516
  102.4 0.6 copy-done.5
  103.0 1.5 copy.12
  104.5 1.4 multiply_add_fusion
  105.9 1.5 copy.13
  107.3 1.4 fusion
  108.8 8.7 %cholesky.20 = f32[80,80]{1,0:T(8,128)} custom-call(f32[80,80]{1,0:T(8,128)} %fusion), custom_call_target="Cholesky" | custom-call | tf_op jit(solution)/shard_map/jit(cholesky)/cholesky | solution.py:560
  117.5 1.5 copy.14
  119.0 0.9 select_reduce_fusion
  119.8 0.7 compare_reduce_fusion
  120.6 2.1 %select_bitcast_fusion = f32[80,80]{1,0:T(8,128)} fusion(f32[80,80]{0,1:T(8,128)} %copy.14, pred[]{:T(512)} %compare_reduce_fusion), kind=kLoop, calls=%fused_computation.2 | loop fusion | flops 19200 | bytes 51201 | tf_op jit(solution)/shard_map/transpose | solution.py:560
  122.7 2.5 %copy-done.2 = bf16[80,32,8,128]{3,2,1,0:T(8,128)(2,1)S(1)} copy-done((bf16[80,32,8,128]{3,2,1,0:T(8,128)(2,1)S(1)}, bf16[80,32,8,128]{3,2,1,0:T(8,128)(2,1)}, u32[]{:S(2)}) %copy-start.2) | copy-done | bytes 5242904
  125.1 2.5 %copy-done.4 = bf16[80,32,8,128]{3,2,1,0:T(8,128)(2,1)S(1)} copy-done((bf16[80,32,8,128]{3,2,1,0:T(8,128)(2,1)S(1)}, bf16[80,32,8,128]{3,2,1,0:T(8,128)(2,1)}, u32[]{:S(2)}) %copy-start.4) | copy-done | bytes 5242904
  127.6 21.1 %adjoint.1 = f32[80,256,128]{2,1,0:T(8,128)} custom-call(f32[8]{0:T(128)S(1)} %pad_maximum_fusion.taps_ref, bf16[80,256,128]{2,1,0:T(8,128)(2,1)S(1)} %bitcast.15, bf16[80,256,128]{2,1,0:T(8,128)(2,1)S(1)} %bitcast.18, bf16[80,128,128]{2,1,0:T(8,128)(2,1)S(1)} %get-tuple-element.34.ext_ref, f32[256,128]{1,0:T(8,128)S(1)} %get-tuple-element.35.p_ref, ...), custom_call_target="tpu_custom_call" | custom-call | tf_op jit(solution)/shard_map/adjoint/pallas_call | solution.py:549
  (12 shorter events, 0.0 us)
Async XLA Ops:
  2.0 0.7 copy-start.6
  2.7 0.7 copy-start.7
  3.4 0.7 copy-start.8
  4.1 0.7 copy-start.9
  4.8 0.7 copy-start.10
  8.0 2.5 %copy-start = (bf16[80,32,8,128]{3,2,1,0:T(8,128)(2,1)S(1)}, bf16[80,32,8,128]{3,2,1,0:T(8,128)(2,1)}, u32[]{:S(2)}) copy-start(bf16[80,32,8,128]{3,2,1,0:T(8,128)(2,1)} %param.10) | copy-start | bytes 15728644
  10.4 2.5 %copy-start.3 = (bf16[80,32,8,128]{3,2,1,0:T(8,128)(2,1)S(1)}, bf16[80,32,8,128]{3,2,1,0:T(8,128)(2,1)}, u32[]{:S(2)}) copy-start(bf16[80,32,8,128]{3,2,1,0:T(8,128)(2,1)} %param.11) | copy-start | bytes 15728644
  12.9 16.5 %copy-start.1 = (bf16[80,32,8,128]{3,2,1,0:T(8,128)(2,1)S(1)}, bf16[80,32,8,128]{3,2,1,0:T(8,128)(2,1)}, u32[]{:S(2)}) copy-start(bf16[80,32,8,128]{3,2,1,0:T(8,128)(2,1)} %param.10) | copy-start | bytes 15728644
  102.4 0.6 copy-start.5
  122.7 2.5 %copy-start.2 = (bf16[80,32,8,128]{3,2,1,0:T(8,128)(2,1)S(1)}, bf16[80,32,8,128]{3,2,1,0:T(8,128)(2,1)}, u32[]{:S(2)}) copy-start(bf16[80,32,8,128]{3,2,1,0:T(8,128)(2,1)} %param.10) | copy-start | bytes 15728644
  125.1 2.5 %copy-start.4 = (bf16[80,32,8,128]{3,2,1,0:T(8,128)(2,1)S(1)}, bf16[80,32,8,128]{3,2,1,0:T(8,128)(2,1)}, u32[]{:S(2)}) copy-start(bf16[80,32,8,128]{3,2,1,0:T(8,128)(2,1)} %param.11) | copy-start | bytes 15728644

commit v2 on v1

v2 whole, which is shorter than its diff:
```python
import functools

import jax
import jax.numpy as jnp
from jax import lax
from jax.experimental import pallas as pl
from jax.experimental.pallas import tpu as pltpu
from jax.sharding import PartitionSpec as P

OFFSETS = (-2, -1, 1, 2)
F32, BF = jnp.float32, jnp.bfloat16
MIB = 1024 * 1024
MESH = pl.DeviceIdType.MESH


def nn(a, b):
    return jnp.dot(a, b, preferred_element_type=F32)


def nt(a, b):
    return lax.dot_general(a, b, (((1,), (1,)), ((), ())), preferred_element_type=F32)


def tn(a, b):
    return lax.dot_general(a, b, (((0,), (0,)), ((), ())), preferred_element_type=F32)


def split(x):
    hi = x.astype(BF)
    return hi, (x - hi.astype(F32)).astype(BF)


def iota(shape, axis):
    return lax.broadcasted_iota(jnp.int32, shape, axis)


def band(diff, taps_ref, sign):
    out = jnp.where(diff == 0, 1.0, 0.0)
    for t, offset in enumerate(OFFSETS):
        out = out + jnp.where(diff == sign * offset, taps_ref[t], 0.0)
    return out


def halo_place(h, levels, cols):
    side = h // (2 * levels)
    rest = h - side * 2 * levels
    d = rest // levels
    return rest - d * levels, d + side * (cols - 2), d - 2 + side * (cols + 2)


def setup_kernel(dims, lat_taps, lon_taps, count_ref, e_hbm, mix_hbm, place_hbm, keep_hbm, weight_hbm, innov_hbm,
                 e_ref, kf_ref, ka_ref, lf_ref, la_ref, bf_ref, ba_ref, q_ref, v_ref, meta_ref, start_ref,
                 mix_ref, place_ref, keep_ref, weight_ref, innov_ref, sems):
    levels, cols, lanes = dims
    small = [pltpu.make_async_copy(a, b, sems.at[i]) for i, (a, b) in enumerate(
        ((mix_hbm, mix_ref), (place_hbm, place_ref), (keep_hbm, keep_ref), (weight_hbm, weight_ref),
         (innov_hbm, innov_ref)))]
    large = pltpu.make_async_copy(e_hbm, e_ref, sems.at[5])
    for copy in small:
        copy.start()
    large.start()
    rows, half = levels * cols, 2 * levels
    ext = rows + 2 * half

    def ext_level_col(x):
        k, own, outer = halo_place(x - rows, levels, cols)
        inside = x < rows
        xk = x // cols
        return jnp.where(inside, xk, k), jnp.where(inside, x - xk * cols, own), jnp.where(
            inside, x - xk * cols, outer)

    diff = iota((lanes, lanes), 0) - iota((lanes, lanes), 1)
    lf_ref[...] = jnp.concatenate(split(band(diff, lat_taps, 1)), axis=0)
    la_ref[...] = jnp.concatenate(split(band(diff, lat_taps, -1)), axis=0)
    src, dst = iota((lanes, lanes), 0), iota((lanes, lanes), 1)
    member = (src // 4) == (dst // 4)
    t, u = src % 4, dst % 4
    at = jnp.where(t < 2, t - 2, lanes + t - 2) - jnp.where(u < 2, lanes - 2 + u, u - 2)
    bf_ref[...] = jnp.concatenate(split(jnp.where(member, band(at, lat_taps, 1), 0.0)), axis=0)
    ba_ref[...] = jnp.concatenate(split(jnp.where(member, band(at, lat_taps, -1), 0.0)), axis=0)
    for copy in small:
        copy.wait()
    mix = mix_ref[...]
    level, _, col = ext_level_col(iota((ext, rows), 0))
    y = iota((ext, rows), 1)
    taps = band((y - y // cols * cols) - col, lon_taps, 1)
    pick = (ext_level_col(iota((ext, levels), 0))[0] == iota((ext, levels), 1)).astype(F32).astype(BF)
    put = (iota((levels, rows), 1) // cols == iota((levels, rows), 0)).astype(F32).astype(BF)
    hi, lo = split(nn(nn(pick, mix).astype(BF), put) * taps)
    kf_ref[:ext] = hi
    kf_ref[ext:] = lo
    level, _, col = ext_level_col(iota((rows, ext), 1))
    y = iota((rows, ext), 0)
    taps = band((y - y // cols * cols) - col, lon_taps, 1)
    pick = (ext_level_col(iota((levels, ext), 1))[0] == iota((levels, ext), 0)).astype(F32).astype(BF)
    put = (iota((rows, levels), 0) // cols == iota((rows, levels), 1)).astype(F32).astype(BF)
    hi, lo = split(nn(put, nn(mix.T, pick).astype(BF)) * taps)
    ka_ref[:rows] = hi
    ka_ref[rows:] = lo
    slots = place_ref.shape[1]
    chunk = 512 if slots % 512 == 0 else slots
    ids = iota((ext, chunk), 0)
    ids_level, ids_col, _ = ext_level_col(iota((ext, 1), 0))
    ids = jnp.broadcast_to(ids_level * cols + ids_col, (ext, chunk))
    lane_ids = iota((lanes, chunk), 0)
    total = jnp.zeros((ext, 4 * lanes), F32)
    for s in range(0, slots, chunk):
        place = place_ref[:, s : s + chunk]
        r = place // lanes
        c = place - r * lanes
        live = (iota((1, chunk), 1) + s < count_ref[0, 0]).astype(F32) * keep_ref[:, s : s + chunk].astype(F32)
        q = live * weight_ref[:, s : s + chunk]
        v = q * innov_ref[:, s : s + chunk]
        hit = lane_ids == c
        parts = []
        for x in (q, v):
            for part in split(x):
                parts.append(jnp.where(hit, part.astype(F32), 0.0).astype(BF))
        total = total + nt((ids == r).astype(F32).astype(BF), jnp.concatenate(parts, axis=0))
    q = total[:, :lanes] + total[:, lanes : 2 * lanes]
    v = total[:, 2 * lanes : 3 * lanes] + total[:, 3 * lanes :]
    q_ref[...] = q[:rows]
    v_ref[...] = v[:rows]
    held = q[rows:] > 0.0
    occupied = held.astype(F32).astype(BF)
    n = 2 * half
    before = (iota((lanes, lanes), 0) < iota((lanes, lanes), 1)).astype(F32).astype(BF)
    above = (iota((n, n), 1) < iota((n, n), 0)).astype(F32).astype(BF)
    within = nn(occupied, before)
    start = nn(above, nn(occupied, jnp.ones((lanes, lanes), BF)).astype(BF))
    rank = (start + within).astype(jnp.int32)
    last = max(slots // lanes - 1, 0)
    block = jnp.minimum(start.astype(jnp.int32) // lanes, last)
    relative = jnp.where(held, rank - block * lanes, -1)
    count = nt(jnp.ones((8, lanes), BF), occupied).astype(BF)
    below = (iota((n, n), 0) < iota((n, n), 1)).astype(F32).astype(BF)
    start_ref[...] = jnp.minimum(nn(count, below).astype(jnp.int32) // lanes, last)
    for side in range(2):
        at = slice(side * half, (side + 1) * half)
        meta_ref[side, 0] = relative[at].astype(F32)
        meta_ref[side, 1] = q[rows:][at]
        meta_ref[side, 2] = v[rows:][at]
    large.wait()


def spot(relative_row, width):
    lanes = relative_row.shape[1]
    ranks = iota((width, lanes), 0).astype(F32)
    return jnp.where(jnp.broadcast_to(relative_row, (width, lanes)) == ranks, 1.0, 0.0).astype(BF)


def turn_edges(x, m, at_edge):
    lanes = x.shape[1]
    per = lanes // 4
    return pltpu.roll(jnp.where(at_edge, x, 0.0), lax.rem(2 + 4 * (m - m // per * per), lanes), 1)


def load_rows(ref, j, members, stride):
    return ref[pl.ds(j, members, stride=stride), :]


def gather_kernel(dims, start_ref, c_hbm, e_ref, meta_ref, c_ref, packed_ref, wide_ref, sum_ref, sem):
    levels, cols, lanes = dims
    members = e_ref.shape[0]
    half = 2 * levels
    per = 2
    pitch = per * cols + 8
    copy = pltpu.make_async_copy(c_hbm, c_ref, sem)
    copy.start()
    sum_ref[...] = jnp.zeros_like(sum_ref)

    def body(g, _):
        base = pl.multiple_of(g * per * cols, per * cols)
        x = e_ref[:, pl.ds(base, per * cols), :].astype(F32)
        for m in range(members):
            wide_ref[m * pitch : m * pitch + per * cols, :] = x[m]
        found = []
        for j in range(per * cols):
            col = j % cols
            if 2 <= col < cols - 2:
                continue
            side = int(col >= 2)
            h = (col - side * (cols - 2)) * levels + g * per + j // cols
            xb = load_rows(wide_ref, j, members, pitch).astype(BF)
            got = nt(xb, spot(meta_ref[side, 0, pl.ds(h, 1), :], 2 * lanes))
            found.append((start_ref[0, side * half + h], got))
        for b, got in found:
            sum_ref[b] += got[:, :lanes]
            sum_ref[b + 1] += got[:, lanes:]
        return 0

    lax.fori_loop(0, levels // per, body, 0)
    for b in range(packed_ref.shape[0]):
        packed_ref[b] = sum_ref[b].astype(BF)
    copy.wait()


def factor(s_ref, out_ref, size):
    lanes = s_ref.shape[1]
    step = 8
    lane = iota((step, lanes), 1)
    row = iota((step, lanes), 0)
    for b in range(0, size, step):
        panel = s_ref[b : b + step, :]
        cols = [jnp.broadcast_to(panel[:, b + i : b + i + 1], (step, lanes)) for i in range(step)]
        done = jnp.zeros((step, lanes), F32)
        for j in range(step):
            scale = lax.rsqrt(jnp.broadcast_to(cols[j][j : j + 1], (step, lanes)))
            across = jnp.broadcast_to(panel[j : j + 1], (step, lanes)) * scale
            done = jnp.where(row == j, across, done)
            down = cols[j] * scale
            panel = panel - down * across
            for i in range(j + 1, step):
                cols[i] = cols[i] - down * jnp.broadcast_to(down[i : i + 1], (step, lanes))
        done = jnp.where(lane >= b + row, done, 0.0)
        out_ref[b : b + step, :] = done[:, :size]
        if b + step < size:
            hi, lo = split(done)
            low = jnp.concatenate([hi, hi, lo], axis=0)
            high = jnp.concatenate([hi, lo, hi], axis=0)
            s_ref[...] = s_ref[...] - tn(low, high)[:size]


def exchange_kernel(dims, sizes, lat_taps, c_ref, e_ref, q_ref, v_ref, kf_ref, lf_ref, bf_ref, packed_ref, meta_ref,
                    start_ref,
                    p_ref, px_ref, ext_ref, edge_ref, upper_ref,
                    got_left, got_right, got_meta, got_start, start_smem, own_c, own_e, lat_c, lat_e, lat_x, own_x, outer_ref,
                    inc_ref, wide_ref, send_inc, got_inc, p_edge, got_edge, gram_in, total_ref, given_ref,
                    far_sem, far_recv, lat_sem, lat_recv, x_sem, x_recv, inc_sem, inc_recv,
                    pe_sem, pe_recv, gram_sem, gram_recv, smem_sem):
    levels, cols, lanes = dims
    n_lat, n_lon = sizes
    members, rows = c_ref.shape[0], c_ref.shape[1]
    half = 2 * levels
    ext = rows + 2 * half
    per = lanes // 4
    groups = own_e.shape[0]
    lat, lon = lax.axis_index("lat"), lax.axis_index("lon")
    left, right = lax.rem(lon + n_lon - 1, n_lon), lax.rem(lon + 1, n_lon)
    has_before, has_after = lat > 0, lat < n_lat - 1

    def flip(x, bit):
        return x + bit - 2 * bit * (x // bit - x // (2 * bit) * 2)

    partners = [("lat", 1 << i) for i in range(n_lat.bit_length() - 1)]
    n_near = len(partners)
    partners += [("lon", 1 << i) for i in range(n_lon.bit_length() - 1)]
    barrier = pltpu.get_barrier_semaphore()

    def greet(where):
        pl.semaphore_signal(barrier, inc=1, device_id=where, device_id_type=MESH)

    greet({"lon": left})
    greet({"lon": right})

    @pl.when(has_before)
    def _():
        greet({"lat": lat - 1})

    @pl.when(has_after)
    def _():
        greet({"lat": lat + 1})

    for axis, bit in partners:
        greet({axis: flip(lat if axis == "lat" else lon, bit)})

    lane = iota((rows, lanes), 1)
    at_edge = (lane < 2) | (lane >= lanes - 2)
    for g in range(groups):
        first, last = g * per, min((g + 1) * per, members)

        def pack(k, both, first=first):
            c, e = both
            for i in range(2):
                m = first + 2 * k + i
                c = c + turn_edges(c_ref[m].astype(F32), m, at_edge)
                e = e + turn_edges(e_ref[m].astype(F32), m, at_edge)
            return c, e

        zero = jnp.zeros((rows, lanes), F32)
        c, e = lax.fori_loop(0, (last - first) // 2, pack, (zero, zero))
        own_c[g] = c.astype(BF)
        own_e[g] = e.astype(BF)

    pl.semaphore_wait(barrier, 2 + len(partners) + has_before.astype(jnp.int32) + has_after.astype(jnp.int32))

    def remote(src, dst, s, r, where):
        return pltpu.make_async_remote_copy(
            src_ref=src, dst_ref=dst, send_sem=s, recv_sem=r, device_id=where, device_id_type=MESH)

    blocks = packed_ref.shape[0]
    got = (got_left, got_right)
    far = []
    for slot, to in ((0, right), (1, left)):
        mine = 1 - slot
        far.append([
            remote(meta_ref.at[mine], got_meta.at[slot], far_sem.at[slot, 0], far_recv.at[slot, 0], {"lon": to}),
            remote(start_ref, got_start.at[slot], far_sem.at[slot, 1], far_recv.at[slot, 1], {"lon": to}),
            remote(packed_ref, got[slot].at[pl.ds(0, blocks)], far_sem.at[slot, 2], far_recv.at[slot, 2],
                   {"lon": to})])

    def lat_pair(src, dst, s, r, k):
        up = remote(src, dst.at[0], s.at[0, k], r.at[0, k], {"lat": lat + 1})
        down = remote(src, dst.at[1], s.at[1, k], r.at[1, k], {"lat": lat - 1})
        return up, down

    def lat_start(up, down):
        pl.when(has_after)(up.start)
        pl.when(has_before)(down.start)

    def lat_wait(up, down):
        pl.when(has_after)(up.wait_send)
        pl.when(has_before)(down.wait_send)
        pl.when(has_before)(up.wait_recv)
        pl.when(has_after)(down.wait_recv)

    near = [lat_pair(own_c, lat_c, lat_sem, lat_recv, 0), lat_pair(own_e, lat_e, lat_sem, lat_recv, 1)]
    for pair in near:
        lat_start(*pair)
    for copies in far:
        for copy in copies:
            copy.start()

    for side, missing in ((0, jnp.logical_not(has_before)), (1, jnp.logical_not(has_after))):
        @pl.when(missing)
        def _(side=side):
            for ref in (lat_c, lat_e, lat_x, got_edge):
                ref[side] = jnp.zeros_like(ref[side])

    for slot in range(2):
        got[slot][blocks] = jnp.zeros_like(got[slot][blocks])
    inc_ref[...] = jnp.zeros_like(inc_ref)

    two = 2
    pitch = two * cols + 8

    def grams(g, gram):
        base = pl.multiple_of(g * two * cols, two * cols)
        x = e_ref[:, pl.ds(base, two * cols), :].astype(F32)
        for m in range(members):
            wide_ref[m * pitch : m * pitch + two * cols, :] = x[m]
        weight = q_ref[pl.ds(base, two * cols), :]
        for pair in range(0, two * cols, 2):
            plain, his, los = [], [], []
            for j in (pair, pair + 1):
                y = load_rows(wide_ref, j, members, pitch)
                plain.append(y.astype(BF))
                hi, lo = split(y * weight[j : j + 1])
                his.append(hi)
                los.append(lo)
            weighted = jnp.concatenate([jnp.concatenate(his, axis=1), jnp.concatenate(los, axis=1)], axis=0)
            gram = gram + nt(weighted, jnp.concatenate(plain, axis=1))
        return gram

    gram = lax.fori_loop(0, levels // two, grams, jnp.zeros((2 * members, members), F32))
    total_ref[...] = jnp.zeros_like(total_ref)
    total_ref[:, :members] = gram[:members] + gram[members:]

    stages = []

    def stage_start():
        i = len(stages)
        if i < len(partners):
            axis, bit = partners[i]
            gram_in[i, 0] = total_ref[...]
            copy = remote(gram_in.at[i, 0], gram_in.at[i, 1], gram_sem.at[i], gram_recv.at[i],
                          {axis: flip(lat if axis == "lat" else lon, bit)})
            copy.start()
            stages.append(copy)

    def stage_end():
        i = len(stages) - 1
        stages[i].wait()
        total_ref[...] = total_ref[...] + gram_in[i, 1]

    def forward(pair, _):
        x = [c_ref[2 * pair + i] for i in range(2)]
        x = jnp.concatenate([jnp.concatenate([y, y], axis=1) for y in x], axis=0)
        y = nn(x, lf_ref[...]).astype(BF)
        out = nn(kf_ref[...], jnp.concatenate([y[:rows], y[rows:]], axis=1))
        out = out[:ext] + out[ext:]
        total = inc_ref[...]
        for i in range(2):
            m = 2 * pair + i
            part = out[:, i * lanes : (i + 1) * lanes]
            total = total + e_ref[m].astype(F32) * part[:rows]
            outer_ref[m] = part[rows:].astype(BF)
        inc_ref[...] = total
        return 0

    pairs = members // 2
    cuts = [pairs * i // (n_near + 1) for i in range(n_near + 2)]
    for i in range(n_near + 1):
        stage_start()
        lax.fori_loop(cuts[i], cuts[i + 1], forward, 0)
        if i < n_near:
            stage_end()

    for pair in near:
        lat_wait(*pair)
    before = iota((rows, lanes), 1) % 4 < 2
    spare = []
    for g in range(groups):
        halo = jnp.where(before, lat_c[0, g].astype(F32), lat_c[1, g].astype(F32)).astype(BF)
        mixed = nn(kf_ref[...], halo)
        mixed = (mixed[:ext] + mixed[ext:]).astype(BF)
        spare.append(nn(jnp.concatenate([mixed, mixed], axis=1), bf_ref[...]))
    source = iota((lanes, lanes), 0) % 4
    target = iota((lanes, lanes), 1)
    drop = (target == jnp.where(source < 2, lanes - 2 + source, source - 2)).astype(F32).astype(BF)

    def settle(products):
        total = None
        for x in products:
            part = nn(jnp.concatenate(split(x), axis=1), jnp.concatenate([drop, drop], axis=0))
            total = part if total is None else total + part
        return total

    inc_ref[...] += settle([own_e[g].astype(F32) * spare[g][:rows] for g in range(groups)])

    pitch_x = 2 * half + 8
    for slot in range(2):
        for copy in far[slot]:
            copy.wait()
        copy = pltpu.make_async_copy(got_start.at[slot], start_smem.at[slot], smem_sem)
        copy.start()
        copy.wait()

        def expand(k, _, slot=slot):
            for i in range(8):
                h = k * 8 + i
                b = start_smem[slot, 0, (1 - slot) * half + h]
                hot = spot(got_meta[slot, 0, pl.ds(h, 1), :], 2 * lanes)
                x = nn(jnp.concatenate([got[slot][b], got[slot][b + 1]], axis=1), hot)
                wide_ref[pl.ds(slot * half + h, members, stride=pitch_x), :] = x
            return 0

        lax.fori_loop(0, half // 8, expand, 0)
        if len(stages) > n_near:
            stage_end()
            stage_start()

    edge_x = at_edge[: 2 * half]
    given_ref[...] = jnp.zeros_like(given_ref)
    for g in range(groups):
        first, last = g * per, min((g + 1) * per, members)

        def outer(k, carry, first=first):
            total, edges = carry
            for i in range(2):
                m = first + 2 * k + i
                x = wide_ref[pl.ds(pl.multiple_of(m * pitch_x, 8), 2 * half), :]
                ext_ref[m] = x.astype(BF)
                total = total + x * outer_ref[m].astype(F32)
                edges = edges + turn_edges(x, m, edge_x)
            return total, edges

        zero = jnp.zeros((2 * half, lanes), F32)
        total, edges = lax.fori_loop(0, (last - first) // 2, outer, (zero, zero))
        given_ref[...] += total
        own_x[g] = edges.astype(BF)
    given_ref[...] += settle([own_x[g].astype(F32) * spare[g][rows:] for g in range(groups)])

    for d in range(2):
        at = slice(d * levels, (d + 1) * levels)
        send_inc[0, 0, at] = inc_ref[pl.ds(cols - 2 + d, levels, stride=cols), :]
        send_inc[1, 0, at] = inc_ref[pl.ds(d, levels, stride=cols), :]
    send_inc[0, 1] = given_ref[half:]
    send_inc[1, 1] = given_ref[:half]
    swap = []
    for slot, to in ((0, right), (1, left)):
        swap.append(remote(send_inc.at[slot], got_inc.at[slot], inc_sem.at[slot], inc_recv.at[slot], {"lon": to}))
    for copy in swap:
        copy.start()
    across = lat_pair(own_x, lat_x, x_sem, x_recv, 0)
    lat_start(*across)

    while True:
        if stages:
            stage_end()
        if len(stages) == len(partners):
            break
        stage_start()
    eye = (iota((members, lanes), 0) == iota((members, lanes), 1)).astype(F32)
    total_obs = packed_ref.shape[0] * lanes * n_lat * n_lon
    total_ref[...] = eye + members / total_obs * total_ref[...]
    factor(total_ref, upper_ref, members)

    for copy in swap:
        copy.wait()
    for slot in range(2):
        px_ref[slot * half : (slot + 1) * half] = (
            got_meta[slot, 1] * (got_inc[slot, 0] + given_ref[slot * half : (slot + 1) * half]) - got_meta[slot, 2])
        for d in range(2):
            at = pl.ds(slot * (cols - 2) + d, levels, stride=cols)
            inc_ref[at, :] = inc_ref[at, :] + got_inc[slot, 1, d * levels : (d + 1) * levels]
    p_ref[...] = q_ref[...] * inc_ref[...] - v_ref[...]

    edge_row, edge_lane = iota((8, lanes), 0), iota((8, lanes), 1)
    pick = jnp.where(edge_lane == jnp.where(edge_row < 2, lanes - 2 + edge_row, edge_row - 2), 1.0, 0.0)
    pick = jnp.where(edge_row < 4, pick, 0.0).astype(BF)
    for ref, at in ((p_ref, slice(0, rows)), (px_ref, slice(rows, ext))):
        hi, lo = split(ref[...])
        p_edge[:, at] = nt(pick, hi) + nt(pick, lo)
    final = lat_pair(p_edge, got_edge, pe_sem, pe_recv, 0)
    lat_start(*final)
    lat_wait(*across)
    before = iota((ext, lanes), 1) % 4 < 2
    halo = []
    for g in range(groups):
        far_e = [jnp.concatenate([lat_e[side, g], lat_x[side, g]], axis=0).astype(F32) for side in range(2)]
        halo.append(jnp.where(before, far_e[0], far_e[1]))
    spread = jnp.where((edge_lane % 4 == edge_row) & (edge_row < 4), 1.0, 0.0).astype(BF)
    lat_wait(*final)
    p_halo = jnp.where(iota((8, ext), 0) < 2, got_edge[0], got_edge[1])
    hi, lo = split(p_halo)
    p_halo = tn(hi, spread) + tn(lo, spread)
    for g in range(groups):
        edge_ref[g] = (halo[g] * p_halo).astype(BF)


def adjoint_kernel(dims, block, c_ref, e_ref, ext_ref, p_ref, px_ref, pe_ref, ka_ref, la_ref, ba_ref, upper_ref,
                   out_ref, upper_out, edge_ref):
    levels, cols, lanes = dims
    members, rows = c_ref.shape[0], c_ref.shape[1]
    step = pl.program_id(0)
    per = lanes // 4

    @pl.when(step == 0)
    def _():
        upper_out[...] = upper_ref[...]
        for g in range(edge_ref.shape[0]):
            z = nn(ka_ref[...], pe_ref[g])
            z = (z[:rows] + z[rows:]).astype(BF)
            edge_ref[g] = nn(jnp.concatenate([z, z], axis=1), ba_ref[...])

    lane = iota((rows, lanes), 1)
    at_edge = (lane < 2) | (lane >= lanes - 2)
    p, px = p_ref[...], px_ref[...]

    for pair in range(block // 2):
        wide = []
        for i in range(2):
            m = step * block + 2 * pair + i
            own = (e_ref[m].astype(F32) * p).astype(BF)
            far = (ext_ref[m].astype(F32) * px).astype(BF)
            wide.append(jnp.concatenate([own, far], axis=0))
        z = nn(ka_ref[...], jnp.concatenate(wide, axis=1))
        z = (z[:rows] + z[rows:]).astype(BF)
        z = jnp.concatenate([z[:, :lanes], z[:, lanes:]], axis=0)
        y = nn(jnp.concatenate([z, z], axis=1), la_ref[...])
        for i in range(2):
            m = step * block + 2 * pair + i
            g = m // per
            turned = pltpu.roll(edge_ref[g], lax.rem(2 * lanes - 2 - 4 * (m - g * per), lanes), 1)
            out_ref[2 * pair + i] = (
                c_ref[m].astype(F32) + y[i * rows : (i + 1) * rows] + jnp.where(at_edge, turned, 0.0))


def shards(
    control, ensemble, level_mix, lat_taps, lon_taps, obs_location, obs_count, obs_keep, innovation, obs_weight
):
    members, levels, cols, lanes = control.shape
    dims = (levels, cols, lanes)
    rows, half = levels * cols, 2 * levels
    ext = rows + 2 * half
    slots = obs_location.shape[2]
    blocks = slots // lanes
    groups = -(-4 * members // lanes)
    n_lat, n_lon = lax.axis_size("lat"), lax.axis_size("lon")
    vm, sm = pl.BlockSpec(memory_space=pltpu.VMEM), pl.BlockSpec(memory_space=pltpu.SMEM)
    hbm = pl.BlockSpec(memory_space=pltpu.HBM)
    dma = pltpu.SemaphoreType.DMA
    away = functools.partial(pltpu.with_memory_space_constraint, memory_space=pltpu.HBM)

    def sds(shape, dtype=F32):
        return jax.ShapeDtypeStruct(shape, dtype)

    e3, kf, ka, lf, la, bf, ba, q, v, meta, start = pl.pallas_call(
        functools.partial(setup_kernel, dims),
        in_specs=[sm, sm, sm] + [hbm] * 6,
        out_specs=[vm] * 11,
        out_shape=[sds((members, rows, lanes), BF), sds((2 * ext, rows), BF), sds((2 * rows, ext), BF)]
        + [sds((2 * lanes, lanes), BF)] * 4
        + [sds((rows, lanes)), sds((rows, lanes)), sds((2, 3, half, lanes)), sds((8, 2 * half), jnp.int32)],
        scratch_shapes=[pltpu.VMEM((levels, levels), BF), pltpu.VMEM((1, slots), jnp.int32),
                        pltpu.VMEM((1, slots), jnp.int32), pltpu.VMEM((1, slots), F32), pltpu.VMEM((1, slots), F32),
                        dma((6,))],
        compiler_params=pltpu.CompilerParams(vmem_limit_bytes=8 * MIB),
        name="setup",
    )(lat_taps, lon_taps, obs_count, away(ensemble.reshape(members, rows, lanes)), away(level_mix),
      away(obs_location[0]), away(obs_keep[0]), away(obs_weight[0]), away(innovation[0]))

    c3, packed = pl.pallas_call(
        functools.partial(gather_kernel, dims),
        in_specs=[sm, hbm, vm, vm],
        out_specs=[vm] * 2,
        out_shape=[sds((members, rows, lanes), BF), sds((blocks, members, lanes), BF)],
        scratch_shapes=[pltpu.VMEM((members * (2 * cols + 8), lanes), F32),
                        pltpu.VMEM((blocks + 1, members, lanes), F32), dma],
        compiler_params=pltpu.CompilerParams(vmem_limit_bytes=8 * MIB),
        name="gather",
    )(start, away(control.reshape(members, rows, lanes)), e3, meta)

    n_bits = (n_lat.bit_length() - 1) + (n_lon.bit_length() - 1)
    p, px, e_ext, p_edge, upper = pl.pallas_call(
        functools.partial(exchange_kernel, dims, (n_lat, n_lon)),
        in_specs=[sm] + [vm] * 10,
        out_specs=[vm] * 5,
        out_shape=[sds((rows, lanes)), sds((2 * half, lanes)), sds((members, 2 * half, lanes), BF),
                   sds((groups, ext, lanes), BF), sds((members, members))],
        scratch_shapes=[
            pltpu.VMEM((blocks + 1, members, lanes), BF),
            pltpu.VMEM((blocks + 1, members, lanes), BF),
            pltpu.VMEM((2, 3, half, lanes), F32),
            pltpu.VMEM((2, 8, 2 * half), jnp.int32),
            pltpu.SMEM((2, 8, 2 * half), jnp.int32),
            pltpu.VMEM((groups, rows, lanes), BF),
            pltpu.VMEM((groups, rows, lanes), BF),
            pltpu.VMEM((2, groups, rows, lanes), BF),
            pltpu.VMEM((2, groups, rows, lanes), BF),
            pltpu.VMEM((2, groups, 2 * half, lanes), BF),
            pltpu.VMEM((groups, 2 * half, lanes), BF),
            pltpu.VMEM((members, 2 * half, lanes), BF),
            pltpu.VMEM((rows, lanes), F32),
            pltpu.VMEM((members * (2 * half + 8), lanes), F32),
            pltpu.VMEM((2, 2, half, lanes), F32),
            pltpu.VMEM((2, 2, half, lanes), F32),
            pltpu.VMEM((8, ext), F32),
            pltpu.VMEM((2, 8, ext), F32),
            pltpu.VMEM((n_bits, 2, members, lanes), F32),
            pltpu.VMEM((members, lanes), F32),
            pltpu.VMEM((2 * half, lanes), F32),
            dma((2, 3)), dma((2, 3)), dma((2, 2)), dma((2, 2)), dma((2, 1)), dma((2, 1)), dma((2,)), dma((2,)),
            dma((2, 1)), dma((2, 1)), dma((n_bits,)), dma((n_bits,)), dma,
        ],
        compiler_params=pltpu.CompilerParams(
            vmem_limit_bytes=16 * MIB, collective_id=0, has_side_effects=True),
        name="exchange",
    )(lat_taps, c3, e3, q, v, kf, lf, bf, packed, meta, start)

    block = 8 if members % 8 == 0 else 2
    gradient, upper = pl.pallas_call(
        functools.partial(adjoint_kernel, dims, block),
        grid=(members // block,),
        in_specs=[vm] * 10,
        out_specs=[pl.BlockSpec((block, rows, lanes), lambda g: (g, 0, 0)),
                   pl.BlockSpec((members, members), lambda g: (0, 0))],
        out_shape=[sds((members, rows, lanes)), sds((members, members))],
        scratch_shapes=[pltpu.VMEM((groups, rows, lanes), F32)],
        compiler_params=pltpu.CompilerParams(vmem_limit_bytes=8 * MIB),
        name="adjoint",
    )(c3, e3, e_ext, p, px, p_edge, ka, la, ba, upper)
    return gradient.reshape(members, levels, cols, lanes), upper


def solution(mesh):
    in_specs = (
        P(None, None, "lon", "lat"),
        P(None, None, "lon", "lat"),
        P(),
        P(),
        P(),
        P("lon", "lat", None),
        P("lon", "lat"),
        P("lon", "lat", None),
        P("lon", "lat", None),
        P("lon", "lat", None),
    )
    out_specs = (P(None, None, "lon", "lat"), P())
    return jax.shard_map(shards, mesh=mesh, in_specs=in_specs, out_specs=out_specs, check_vma=False)
```

time: 150 us -> 94.9 us (0.63)
  Pallas kernels: 113 us -> 92 us
  local copies, waits for them, and re-layouts: 18.5 us -> 1.31 us
  other arithmetic: 16 us -> 0 us
    unnamed x22 -> x6, local copies, waits for them, and re-layouts: 14.1 us -> 1.31 us
    pallas_call x1, Pallas kernels: 72.9 us -> 60.3 us  [shards(): pl.pallas_call(functools.partial(exchange_kernel, dims, (n_lat, n_lon)),...]
    another operation x3 -> x0, other arithmetic: 10.3 us -> none  [shards(): jnp.linalg.cholesky(jnp.eye(members, dtype=F32) + members / total_obs * g...]
    pallas_call x2, Pallas kernels: 18.9 us -> 9.45 us  [the longest x1 6.24 us: shards(): pl.pallas_call(functools.partial(gather_kernel, dims), in_specs=[sm, hbm,...]
    transpose x1 -> x0, other arithmetic: 2.09 us -> none  [shards(): jnp.linalg.cholesky(jnp.eye(members, dtype=F32) + members / total_obs * g...]
where the time goes in v2:
time: 94.9 us; the launch traced here: 94.6 us
  Pallas kernels  92 us (97%)
  between operations  1.33 us (1%)
  local copies, waits for them, and re-layouts  1.31 us (1%)
    pallas_call x1, Pallas kernels, shards(): pl.pallas_call(functools.partial(exchange_kernel, dims, (n_lat, n_lon)),...  60.3 us
    pallas_call x1, Pallas kernels, shards(): pl.pallas_call(functools.partial(adjoint_kernel, dims, block), grid=(memb...  22.2 us
    pallas_call x1, Pallas kernels, shards(): pl.pallas_call(functools.partial(gather_kernel, dims), in_specs=[sm, hbm,...  6.24 us
    pallas_call x1, Pallas kernels, shards(): pl.pallas_call(functools.partial(setup_kernel, dims), in_specs=[sm, sm, s...  3.21 us

profile of v2, /device:TPU:1, one launch (start us, length us, event | category | flops | bytes accessed | tf_op | source)
XLA Modules:
  0.0 94.6 jit_solution(12230616205330757630)
XLA Ops:
  1.3 0.0 copy-start
  1.3 0.6 copy-done
  1.9 0.0 copy-start.2
  1.9 0.7 copy-done.2
  2.6 3.2 %setup.1 = (bf16[80,256,128]{2,1,0:T(8,128)(2,1)S(1)}, bf16[768,256]{1,0:T(8,128)(2,1)S(1)}, bf16[512,384]{1,0:T(8,128)(2,1)S(1)}, bf16[256,128]{1,0:T(8,128)(2,...) custom-call(f32[4]{0:T(128)S(1)} %copy-done, ...), custom_call_target="tpu_custom_call" | custom-call | tf_op jit(solution)/shard_map/setup/pallas_call | solution.py:579
  5.8 0.0 copy-start.1
  5.8 6.2 %gather.1 = (bf16[80,256,128]{2,1,0:T(8,128)(2,1)S(1)}, bf16[16,80,128]{2,1,0:T(8,128)(2,1)S(1)}) custom-call(s32[8,128]{1,0:T(8,128)S(1)} %get-tuple-element.22.start_ref, bf16[80,256,128]{2,1,0:T(8,128)(2,1)} %bitcast.8, bf16[80,256,128]{2,1,0:T(8,128)(2,1)S(1)} %get-tuple-element.23.e_ref, f32[2,3,64,128]{3,2,1,0:T(8,128)S(1)} %get-tuple-element.24.meta_ref), custom_call_target="tpu_custom_call" | custom-call | tf_op jit(solution)/shard_map/gather/pallas_call | solution.py:594
  12.1 0.0 copy-done.1
  12.1 60.3 %exchange.1 = (f32[256,128]{1,0:T(8,128)S(1)}, f32[128,128]{1,0:T(8,128)S(1)}, bf16[80,128,128]{2,1,0:T(8,128)(2,1)S(1)}, bf16[3,384,128]{2,1,0:T(8,128)(2,1)S(1)}, f32[80,80]{1,0:T(8,128)S(1)}) custom-call(f32[4]{0:T(128)S(1)} %copy-done.1, bf16[80,256,128]{2,1,0:T(8,128)(2,1)S(1)} %get-tuple-element.25.c_ref, ...), custom_call_target="tpu_custom_call" | custom-call | tf_op jit(solution)/shard_map/exchange/pallas_call | solution.py:606
  72.4 22.2 %adjoint.1 = (f32[80,256,128]{2,1,0:T(8,128)}, f32[80,80]{1,0:T(8,128)}) custom-call(bf16[80,256,128]{2,1,0:T(8,128)(2,1)S(1)} %get-tuple-element.25.c_ref, bf16[80,256,128]{2,1,0:T(8,128)(2,1)S(1)} %get-tuple-element.23.e_ref, bf16[80,128,128]{2,1,0:T(8,128)(2,1)S(1)} %get-tuple-element.32.ext_ref, f32[256,128]{1,0:T(8,128)S(1)} %get-tuple-element.33.p_ref, ...), custom_call_target="tpu_custom_call" | custom-call | tf_op jit(solution)/shard_map/adjoint/pallas_call | solution.py:643
Async XLA Ops:
  1.3 0.7 copy-start
  1.9 0.7 copy-start.2
  5.8 6.3 %copy-start.1 = (f32[4]{0:T(128)S(1)}, f32[4]{0:T(128)}, u32[]{:S(2)}) copy-start(f32[4]{0:T(128)} %lat_taps.3) | copy-start | bytes 52

commit v3 on v2

--- a/solution.py
+++ b/solution.py
@@ -48,17 +48,19 @@
     return rest - d * levels, d + side * (cols - 2), d - 2 + side * (cols + 2)
 
 
-def setup_kernel(dims, lat_taps, lon_taps, count_ref, e_hbm, mix_hbm, place_hbm, keep_hbm, weight_hbm, innov_hbm,
+def setup_kernel(dims, lat_hbm, lon_hbm, count_ref, e_hbm, mix_hbm, place_hbm, keep_hbm, weight_hbm, innov_hbm,
                  e_ref, kf_ref, ka_ref, lf_ref, la_ref, bf_ref, ba_ref, q_ref, v_ref, meta_ref, start_ref,
-                 mix_ref, place_ref, keep_ref, weight_ref, innov_ref, sems):
+                 mix_ref, place_ref, keep_ref, weight_ref, innov_ref, lat_taps, lon_taps, sems):
     levels, cols, lanes = dims
     small = [pltpu.make_async_copy(a, b, sems.at[i]) for i, (a, b) in enumerate(
         ((mix_hbm, mix_ref), (place_hbm, place_ref), (keep_hbm, keep_ref), (weight_hbm, weight_ref),
-         (innov_hbm, innov_ref)))]
-    large = pltpu.make_async_copy(e_hbm, e_ref, sems.at[5])
+         (innov_hbm, innov_ref), (lat_hbm, lat_taps), (lon_hbm, lon_taps)))]
+    large = pltpu.make_async_copy(e_hbm, e_ref, sems.at[len(small)])
     for copy in small:
         copy.start()
     large.start()
+    for copy in small:
+        copy.wait()
     rows, half = levels * cols, 2 * levels
     ext = rows + 2 * half
 
@@ -78,28 +80,25 @@
     at = jnp.where(t < 2, t - 2, lanes + t - 2) - jnp.where(u < 2, lanes - 2 + u, u - 2)
     bf_ref[...] = jnp.concatenate(split(jnp.where(member, band(at, lat_taps, 1), 0.0)), axis=0)
     ba_ref[...] = jnp.concatenate(split(jnp.where(member, band(at, lat_taps, -1), 0.0)), axis=0)
-    for copy in small:
-        copy.wait()
     mix = mix_ref[...]
-    level, _, col = ext_level_col(iota((ext, rows), 0))
-    y = iota((ext, rows), 1)
+    col = ext_level_col(iota((ext, 1), 0))[2]
+    y = iota((1, rows), 1)
     taps = band((y - y // cols * cols) - col, lon_taps, 1)
-    pick = (ext_level_col(iota((ext, levels), 0))[0] == iota((ext, levels), 1)).astype(F32).astype(BF)
-    put = (iota((levels, rows), 1) // cols == iota((levels, rows), 0)).astype(F32).astype(BF)
+    pick = (ext_level_col(iota((ext, 1), 0))[0] == iota((ext, levels), 1)).astype(F32).astype(BF)
+    put = (iota((1, rows), 1) // cols == iota((levels, rows), 0)).astype(F32).astype(BF)
     hi, lo = split(nn(nn(pick, mix).astype(BF), put) * taps)
     kf_ref[:ext] = hi
     kf_ref[ext:] = lo
-    level, _, col = ext_level_col(iota((rows, ext), 1))
-    y = iota((rows, ext), 0)
+    col = ext_level_col(iota((1, ext), 1))[2]
+    y = iota((rows, 1), 0)
     taps = band((y - y // cols * cols) - col, lon_taps, 1)
-    pick = (ext_level_col(iota((levels, ext), 1))[0] == iota((levels, ext), 0)).astype(F32).astype(BF)
-    put = (iota((rows, levels), 0) // cols == iota((rows, levels), 1)).astype(F32).astype(BF)
+    pick = (ext_level_col(iota((1, ext), 1))[0] == iota((levels, ext), 0)).astype(F32).astype(BF)
+    put = (iota((rows, 1), 0) // cols == iota((rows, levels), 1)).astype(F32).astype(BF)
     hi, lo = split(nn(put, nn(mix.T, pick).astype(BF)) * taps)
     ka_ref[:rows] = hi
     ka_ref[rows:] = lo
     slots = place_ref.shape[1]
     chunk = 512 if slots % 512 == 0 else slots
-    ids = iota((ext, chunk), 0)
     ids_level, ids_col, _ = ext_level_col(iota((ext, 1), 0))
     ids = jnp.broadcast_to(ids_level * cols + ids_col, (ext, chunk))
     lane_ids = iota((lanes, chunk), 0)
@@ -149,12 +148,6 @@
     return jnp.where(jnp.broadcast_to(relative_row, (width, lanes)) == ranks, 1.0, 0.0).astype(BF)
 
 
-def turn_edges(x, m, at_edge):
-    lanes = x.shape[1]
-    per = lanes // 4
-    return pltpu.roll(jnp.where(at_edge, x, 0.0), lax.rem(2 + 4 * (m - m // per * per), lanes), 1)
-
-
 def load_rows(ref, j, members, stride):
     return ref[pl.ds(j, members, stride=stride), :]
 
@@ -163,7 +156,7 @@
     levels, cols, lanes = dims
     members = e_ref.shape[0]
     half = 2 * levels
-    per = 2
+    per = 4
     pitch = per * cols + 8
     copy = pltpu.make_async_copy(c_hbm, c_ref, sem)
     copy.start()
@@ -221,7 +214,36 @@
             s_ref[...] = s_ref[...] - tn(low, high)[:size]
 
 
-def exchange_kernel(dims, sizes, lat_taps, c_ref, e_ref, q_ref, v_ref, kf_ref, lf_ref, bf_ref, packed_ref, meta_ref,
+def stacked(a_ref, x, rows):
+    piece = 128 if rows % 128 == 0 else rows
+    parts = [nn(a_ref[r : r + piece], x) + nn(a_ref[rows + r : rows + r + piece], x) for r in range(0, rows, piece)]
+    return jnp.concatenate(parts, axis=0) if len(parts) > 1 else parts[0]
+
+
+def forward_loop(group, c_ref, e_ref, kf_ref, lf_ref, inc_ref, outer_ref, first, last):
+    rows, lanes = inc_ref.shape
+    ext = rows + outer_ref.shape[1]
+
+    def body(step, _):
+        for quad in range(0, group, 4):
+            at = [group * step + quad + i for i in range(4)]
+            smooth = []
+            for m in at:
+                x = c_ref[m]
+                smooth.append(nn(jnp.concatenate([x, x], axis=1), lf_ref[...]).astype(BF))
+            out = [stacked(kf_ref, jnp.concatenate(smooth[2 * i : 2 * i + 2], axis=1), ext) for i in range(2)]
+            total = inc_ref[...]
+            for i, m in enumerate(at):
+                part = out[i // 2][:, i % 2 * lanes : (i % 2 + 1) * lanes]
+                total = total + e_ref[m].astype(F32) * part[:rows]
+                outer_ref[m] = part[rows:].astype(BF)
+            inc_ref[...] = total
+        return 0
+
+    lax.fori_loop(first, last, body, 0)
+
+
+def exchange_kernel(dims, sizes, c_ref, e_ref, q_ref, v_ref, kf_ref, lf_ref, bf_ref, packed_ref, meta_ref,
                     start_ref,
                     p_ref, px_ref, ext_ref, edge_ref, upper_ref,
                     got_left, got_right, got_meta, got_start, start_smem, own_c, own_e, lat_c, lat_e, lat_x, own_x, outer_ref,
@@ -264,23 +286,17 @@
     for axis, bit in partners:
         greet({axis: flip(lat if axis == "lat" else lon, bit)})
 
-    lane = iota((rows, lanes), 1)
-    at_edge = (lane < 2) | (lane >= lanes - 2)
+    packed_at = iota((rows, lanes), 1) // 4
     for g in range(groups):
         first, last = g * per, min((g + 1) * per, members)
-
-        def pack(k, both, first=first):
-            c, e = both
-            for i in range(2):
-                m = first + 2 * k + i
-                c = c + turn_edges(c_ref[m].astype(F32), m, at_edge)
-                e = e + turn_edges(e_ref[m].astype(F32), m, at_edge)
-            return c, e
-
-        zero = jnp.zeros((rows, lanes), F32)
-        c, e = lax.fori_loop(0, (last - first) // 2, pack, (zero, zero))
-        own_c[g] = c.astype(BF)
-        own_e[g] = e.astype(BF)
+        for ref, own in ((c_ref, own_c), (e_ref, own_e)):
+            def pack(k, x, first=first, ref=ref):
+                for i in range(4):
+                    m = first + 4 * k + i
+                    x = jnp.where(packed_at == m - first, pltpu.roll(ref[m], 2 + 4 * (m - first), 1), x)
+                return x
+
+            own[g] = lax.fori_loop(0, (last - first) // 4, pack, jnp.zeros((rows, lanes), BF))
 
     pl.semaphore_wait(barrier, 2 + len(partners) + has_before.astype(jnp.int32) + has_after.astype(jnp.int32))
 
@@ -335,6 +351,7 @@
     pitch = two * cols + 8
 
     def grams(g, gram):
+        gram = list(gram)
         base = pl.multiple_of(g * two * cols, two * cols)
         x = e_ref[:, pl.ds(base, two * cols), :].astype(F32)
         for m in range(members):
@@ -349,10 +366,13 @@
                 his.append(hi)
                 los.append(lo)
             weighted = jnp.concatenate([jnp.concatenate(his, axis=1), jnp.concatenate(los, axis=1)], axis=0)
-            gram = gram + nt(weighted, jnp.concatenate(plain, axis=1))
-        return gram
-
-    gram = lax.fori_loop(0, levels // two, grams, jnp.zeros((2 * members, members), F32))
+            k = pair // 2 % 2
+            gram[k] = gram[k] + nt(weighted, jnp.concatenate(plain, axis=1))
+        return tuple(gram)
+
+    zero = jnp.zeros((2 * members, members), F32)
+    gram = lax.fori_loop(0, levels // two, grams, (zero, zero))
+    gram = gram[0] + gram[1]
     total_ref[...] = jnp.zeros_like(total_ref)
     total_ref[:, :members] = gram[:members] + gram[members:]
 
@@ -373,26 +393,11 @@
         stages[i].wait()
         total_ref[...] = total_ref[...] + gram_in[i, 1]
 
-    def forward(pair, _):
-        x = [c_ref[2 * pair + i] for i in range(2)]
-        x = jnp.concatenate([jnp.concatenate([y, y], axis=1) for y in x], axis=0)
-        y = nn(x, lf_ref[...]).astype(BF)
-        out = nn(kf_ref[...], jnp.concatenate([y[:rows], y[rows:]], axis=1))
-        out = out[:ext] + out[ext:]
-        total = inc_ref[...]
-        for i in range(2):
-            m = 2 * pair + i
-            part = out[:, i * lanes : (i + 1) * lanes]
-            total = total + e_ref[m].astype(F32) * part[:rows]
-            outer_ref[m] = part[rows:].astype(BF)
-        inc_ref[...] = total
-        return 0
-
-    pairs = members // 2
-    cuts = [pairs * i // (n_near + 1) for i in range(n_near + 2)]
+    group = 8 if members % 8 == 0 else 4
+    cuts = [members // group * i // (n_near + 1) for i in range(n_near + 2)]
     for i in range(n_near + 1):
         stage_start()
-        lax.fori_loop(cuts[i], cuts[i + 1], forward, 0)
+        forward_loop(group, c_ref, e_ref, kf_ref, lf_ref, inc_ref, outer_ref, cuts[i], cuts[i + 1])
         if i < n_near:
             stage_end()
 
@@ -440,25 +445,25 @@
             stage_end()
             stage_start()
 
-    edge_x = at_edge[: 2 * half]
     given_ref[...] = jnp.zeros_like(given_ref)
     for g in range(groups):
         first, last = g * per, min((g + 1) * per, members)
 
         def outer(k, carry, first=first):
             total, edges = carry
-            for i in range(2):
-                m = first + 2 * k + i
+            for i in range(4):
+                m = first + 4 * k + i
                 x = wide_ref[pl.ds(pl.multiple_of(m * pitch_x, 8), 2 * half), :]
-                ext_ref[m] = x.astype(BF)
+                xb = x.astype(BF)
+                ext_ref[m] = xb
                 total = total + x * outer_ref[m].astype(F32)
-                edges = edges + turn_edges(x, m, edge_x)
+                edges = jnp.where(packed_at[: 2 * half] == m - first, pltpu.roll(xb, 2 + 4 * (m - first), 1), edges)
             return total, edges
 
         zero = jnp.zeros((2 * half, lanes), F32)
-        total, edges = lax.fori_loop(0, (last - first) // 2, outer, (zero, zero))
+        total, edges = lax.fori_loop(0, (last - first) // 4, outer, (zero, zero.astype(BF)))
         given_ref[...] += total
-        own_x[g] = edges.astype(BF)
+        own_x[g] = edges
     given_ref[...] += settle([own_x[g].astype(F32) * spare[g][rows:] for g in range(groups)])
 
     for d in range(2):
@@ -538,23 +543,23 @@
     at_edge = (lane < 2) | (lane >= lanes - 2)
     p, px = p_ref[...], px_ref[...]
 
-    for pair in range(block // 2):
+    for quad in range(block // 4):
         wide = []
-        for i in range(2):
-            m = step * block + 2 * pair + i
+        for i in range(4):
+            m = step * block + 4 * quad + i
             own = (e_ref[m].astype(F32) * p).astype(BF)
             far = (ext_ref[m].astype(F32) * px).astype(BF)
             wide.append(jnp.concatenate([own, far], axis=0))
-        z = nn(ka_ref[...], jnp.concatenate(wide, axis=1))
-        z = (z[:rows] + z[rows:]).astype(BF)
-        z = jnp.concatenate([z[:, :lanes], z[:, lanes:]], axis=0)
-        y = nn(jnp.concatenate([z, z], axis=1), la_ref[...])
-        for i in range(2):
-            m = step * block + 2 * pair + i
+        mixed = [stacked(ka_ref, jnp.concatenate(wide[2 * i : 2 * i + 2], axis=1), rows).astype(BF) for i in range(2)]
+        smooth = []
+        for i in range(4):
+            z = mixed[i // 2][:, i % 2 * lanes : (i % 2 + 1) * lanes]
+            smooth.append(nn(jnp.concatenate([z, z], axis=1), la_ref[...]))
+        for i in range(4):
+            m = step * block + 4 * quad + i
             g = m // per
             turned = pltpu.roll(edge_ref[g], lax.rem(2 * lanes - 2 - 4 * (m - g * per), lanes), 1)
-            out_ref[2 * pair + i] = (
-                c_ref[m].astype(F32) + y[i * rows : (i + 1) * rows] + jnp.where(at_edge, turned, 0.0))
+            out_ref[4 * quad + i] = c_ref[m].astype(F32) + smooth[i] + jnp.where(at_edge, turned, 0.0)
 
 
 def shards(
@@ -578,17 +583,17 @@
 
     e3, kf, ka, lf, la, bf, ba, q, v, meta, start = pl.pallas_call(
         functools.partial(setup_kernel, dims),
-        in_specs=[sm, sm, sm] + [hbm] * 6,
+        in_specs=[hbm, hbm, sm] + [hbm] * 6,
         out_specs=[vm] * 11,
         out_shape=[sds((members, rows, lanes), BF), sds((2 * ext, rows), BF), sds((2 * rows, ext), BF)]
         + [sds((2 * lanes, lanes), BF)] * 4
         + [sds((rows, lanes)), sds((rows, lanes)), sds((2, 3, half, lanes)), sds((8, 2 * half), jnp.int32)],
         scratch_shapes=[pltpu.VMEM((levels, levels), BF), pltpu.VMEM((1, slots), jnp.int32),
                         pltpu.VMEM((1, slots), jnp.int32), pltpu.VMEM((1, slots), F32), pltpu.VMEM((1, slots), F32),
-                        dma((6,))],
+                        pltpu.SMEM((4,), F32), pltpu.SMEM((4,), F32), dma((8,))],
         compiler_params=pltpu.CompilerParams(vmem_limit_bytes=8 * MIB),
         name="setup",
-    )(lat_taps, lon_taps, obs_count, away(ensemble.reshape(members, rows, lanes)), away(level_mix),
+    )(away(lat_taps), away(lon_taps), obs_count, away(ensemble.reshape(members, rows, lanes)), away(level_mix),
       away(obs_location[0]), away(obs_keep[0]), away(obs_weight[0]), away(innovation[0]))
 
     c3, packed = pl.pallas_call(
@@ -596,7 +601,7 @@
         in_specs=[sm, hbm, vm, vm],
         out_specs=[vm] * 2,
         out_shape=[sds((members, rows, lanes), BF), sds((blocks, members, lanes), BF)],
-        scratch_shapes=[pltpu.VMEM((members * (2 * cols + 8), lanes), F32),
+        scratch_shapes=[pltpu.VMEM((members * (4 * cols + 8), lanes), F32),
                         pltpu.VMEM((blocks + 1, members, lanes), F32), dma],
         compiler_params=pltpu.CompilerParams(vmem_limit_bytes=8 * MIB),
         name="gather",
@@ -605,7 +610,7 @@
     n_bits = (n_lat.bit_length() - 1) + (n_lon.bit_length() - 1)
     p, px, e_ext, p_edge, upper = pl.pallas_call(
         functools.partial(exchange_kernel, dims, (n_lat, n_lon)),
-        in_specs=[sm] + [vm] * 10,
+        in_specs=[vm] * 10,
         out_specs=[vm] * 5,
         out_shape=[sds((rows, lanes)), sds((2 * half, lanes)), sds((members, 2 * half, lanes), BF),
                    sds((groups, ext, lanes), BF), sds((members, members))],
@@ -637,9 +642,9 @@
         compiler_params=pltpu.CompilerParams(
             vmem_limit_bytes=16 * MIB, collective_id=0, has_side_effects=True),
         name="exchange",
-    )(lat_taps, c3, e3, q, v, kf, lf, bf, packed, meta, start)
-
-    block = 8 if members % 8 == 0 else 2
+    )(c3, e3, q, v, kf, lf, bf, packed, meta, start)
+
+    block = 8 if members % 8 == 0 else 4
     gradient, upper = pl.pallas_call(
         functools.partial(adjoint_kernel, dims, block),
         grid=(members // block,),

time: 94.9 us -> 67.4 us (0.71)
  Pallas kernels: 92 us -> 65.9 us
  local copies, waits for them, and re-layouts: 1.31 us -> 0 us
    pallas_call x1, Pallas kernels: 60.3 us -> 44.6 us  [shards(): pl.pallas_call(functools.partial(exchange_kernel, dims, (n_lat, n_lon)),...]
    pallas_call x1, Pallas kernels: 22.2 us -> 13.1 us  [shards(): pl.pallas_call(functools.partial(adjoint_kernel, dims, block), grid=(memb...]
    unnamed x6 -> x0, local copies, waits for them, and re-layouts: 1.31 us -> none
    pallas_call x1, Pallas kernels: 6.24 us -> 5.22 us  [shards(): pl.pallas_call(functools.partial(gather_kernel, dims), in_specs=[sm, hbm,...]
where the time goes in v3:
time: 67.4 us; the launch traced here: 67.2 us
  Pallas kernels  65.9 us (98%)
  between operations  1.3 us (2%)
    pallas_call x1, Pallas kernels, shards(): pl.pallas_call(functools.partial(exchange_kernel, dims, (n_lat, n_lon)),...  44.6 us
    pallas_call x1, Pallas kernels, shards(): pl.pallas_call(functools.partial(adjoint_kernel, dims, block), grid=(memb...  13.1 us
    pallas_call x1, Pallas kernels, shards(): pl.pallas_call(functools.partial(gather_kernel, dims), in_specs=[sm, hbm,...  5.22 us
    pallas_call x1, Pallas kernels, shards(): pl.pallas_call(functools.partial(setup_kernel, dims), in_specs=[hbm, hbm,...  2.91 us

profile of v3, /device:TPU:1, one launch (start us, length us, event | category | flops | bytes accessed | tf_op | source)
XLA Modules:
  0.0 67.2 jit_solution(3365688040654344503)
XLA Ops:
  1.3 2.9 %setup.1 = (bf16[80,256,128]{2,1,0:T(8,128)(2,1)S(1)}, bf16[768,256]{1,0:T(8,128)(2,1)S(1)}, bf16[512,384]{1,0:T(8,128)(2,1)S(1)}, bf16[256,128]{1,0:T(8,128)(2,...) custom-call(f32[4]{0:T(128)} %lat_hbm.1, ...), custom_call_target="tpu_custom_call" | custom-call | tf_op jit(solution)/shard_map/setup/pallas_call | solution.py:584
  4.2 5.2 %gather.1 = (bf16[80,256,128]{2,1,0:T(8,128)(2,1)S(1)}, bf16[16,80,128]{2,1,0:T(8,128)(2,1)S(1)}) custom-call(s32[8,128]{1,0:T(8,128)S(1)} %get-tuple-element.22.start_ref, bf16[80,256,128]{2,1,0:T(8,128)(2,1)} %bitcast.8, bf16[80,256,128]{2,1,0:T(8,128)(2,1)S(1)} %get-tuple-element.23.e_ref, f32[2,3,64,128]{3,2,1,0:T(8,128)S(1)} %get-tuple-element.24.meta_ref), custom_call_target="tpu_custom_call" | custom-call | tf_op jit(solution)/shard_map/gather/pallas_call | solution.py:599
  9.4 44.6 %exchange.1 = (f32[256,128]{1,0:T(8,128)S(1)}, f32[128,128]{1,0:T(8,128)S(1)}, bf16[80,128,128]{2,1,0:T(8,128)(2,1)S(1)}, bf16[3,384,128]{2,1,0:T(8,128)(2,1)S(1)}, f32[80,80]{1,0:T(8,128)S(1)}) custom-call(bf16[80,256,128]{2,1,0:T(8,128)(2,1)S(1)} %get-tuple-element.25.c_ref, bf16[80,256,128]{2,1,0:T(8,128)(2,1)S(1)} %get-tuple-element.23.e_ref, ...), custom_call_target="tpu_custom_call" | custom-call | tf_op jit(solution)/shard_map/exchange/pallas_call | solution.py:611
  54.0 13.1 %adjoint.1 = (f32[80,256,128]{2,1,0:T(8,128)}, f32[80,80]{1,0:T(8,128)}) custom-call(bf16[80,256,128]{2,1,0:T(8,128)(2,1)S(1)} %get-tuple-element.25.c_ref, bf16[80,256,128]{2,1,0:T(8,128)(2,1)S(1)} %get-tuple-element.23.e_ref, bf16[80,128,128]{2,1,0:T(8,128)(2,1)S(1)} %get-tuple-element.32.ext_ref, f32[256,128]{1,0:T(8,128)S(1)} %get-tuple-element.33.p_ref, ...), custom_call_target="tpu_custom_call" | custom-call | tf_op jit(solution)/shard_map/adjoint/pallas_call | solution.py:648

commit v4 on v3

--- a/solution.py
+++ b/solution.py
@@ -10,6 +10,7 @@
 OFFSETS = (-2, -1, 1, 2)
 F32, BF = jnp.float32, jnp.bfloat16
 MIB = 1024 * 1024
+BLOCK = 16
 MESH = pl.DeviceIdType.MESH
 
 
@@ -86,17 +87,13 @@
     taps = band((y - y // cols * cols) - col, lon_taps, 1)
     pick = (ext_level_col(iota((ext, 1), 0))[0] == iota((ext, levels), 1)).astype(F32).astype(BF)
     put = (iota((1, rows), 1) // cols == iota((levels, rows), 0)).astype(F32).astype(BF)
-    hi, lo = split(nn(nn(pick, mix).astype(BF), put) * taps)
-    kf_ref[:ext] = hi
-    kf_ref[ext:] = lo
+    kf_ref[...] = (nn(nn(pick, mix).astype(BF), put) * taps).astype(BF)
     col = ext_level_col(iota((1, ext), 1))[2]
     y = iota((rows, 1), 0)
     taps = band((y - y // cols * cols) - col, lon_taps, 1)
     pick = (ext_level_col(iota((1, ext), 1))[0] == iota((levels, ext), 0)).astype(F32).astype(BF)
     put = (iota((rows, 1), 0) // cols == iota((rows, levels), 1)).astype(F32).astype(BF)
-    hi, lo = split(nn(put, nn(mix.T, pick).astype(BF)) * taps)
-    ka_ref[:rows] = hi
-    ka_ref[rows:] = lo
+    ka_ref[...] = (nn(put, nn(mix.T, pick).astype(BF)) * taps).astype(BF)
     slots = place_ref.shape[1]
     chunk = 512 if slots % 512 == 0 else slots
     ids_level, ids_col, _ = ext_level_col(iota((ext, 1), 0))
@@ -124,19 +121,14 @@
     occupied = held.astype(F32).astype(BF)
     n = 2 * half
     before = (iota((lanes, lanes), 0) < iota((lanes, lanes), 1)).astype(F32).astype(BF)
-    above = (iota((n, n), 1) < iota((n, n), 0)).astype(F32).astype(BF)
     within = nn(occupied, before)
-    start = nn(above, nn(occupied, jnp.ones((lanes, lanes), BF)).astype(BF))
-    rank = (start + within).astype(jnp.int32)
-    last = max(slots // lanes - 1, 0)
-    block = jnp.minimum(start.astype(jnp.int32) // lanes, last)
-    relative = jnp.where(held, rank - block * lanes, -1)
+    relative = jnp.where(held, within, -2.0 * lanes)
     count = nt(jnp.ones((8, lanes), BF), occupied).astype(BF)
     below = (iota((n, n), 0) < iota((n, n), 1)).astype(F32).astype(BF)
-    start_ref[...] = jnp.minimum(nn(count, below).astype(jnp.int32) // lanes, last)
+    start_ref[...] = nn(count, below).astype(jnp.int32)
     for side in range(2):
         at = slice(side * half, (side + 1) * half)
-        meta_ref[side, 0] = relative[at].astype(F32)
+        meta_ref[side, 0] = relative[at]
         meta_ref[side, 1] = q[rows:][at]
         meta_ref[side, 2] = v[rows:][at]
     large.wait()
@@ -152,15 +144,18 @@
     return ref[pl.ds(j, members, stride=stride), :]
 
 
-def gather_kernel(dims, start_ref, c_hbm, e_ref, meta_ref, c_ref, packed_ref, wide_ref, sum_ref, sem):
+def gather_kernel(dims, start_ref, c_hbm, e_ref, meta_ref, c_ref, packed_ref, wide_ref, *rest):
     levels, cols, lanes = dims
     members = e_ref.shape[0]
     half = 2 * levels
     per = 4
     pitch = per * cols + 8
+    sums, sem = rest[:4], rest[4]
     copy = pltpu.make_async_copy(c_hbm, c_ref, sem)
     copy.start()
-    sum_ref[...] = jnp.zeros_like(sum_ref)
+    for ref in sums:
+        ref[...] = jnp.zeros_like(ref)
+    lane = iota((members, lanes), 1)
 
     def body(g, _):
         base = pl.multiple_of(g * per * cols, per * cols)
@@ -175,16 +170,19 @@
             side = int(col >= 2)
             h = (col - side * (cols - 2)) * levels + g * per + j // cols
             xb = load_rows(wide_ref, j, members, pitch).astype(BF)
-            got = nt(xb, spot(meta_ref[side, 0, pl.ds(h, 1), :], 2 * lanes))
-            found.append((start_ref[0, side * half + h], got))
-        for b, got in found:
-            sum_ref[b] += got[:, :lanes]
-            sum_ref[b + 1] += got[:, lanes:]
+            got = nt(xb, spot(meta_ref[side, 0, pl.ds(h, 1), :], lanes))
+            first = start_ref[0, side * half + h]
+            b = first // lanes
+            found.append((sums[2 * side + col - side * (cols - 2)], b, first - b * lanes, got))
+        for sum_ref, b, shift, got in found:
+            got = pltpu.roll(got, shift, 1)
+            sum_ref[b] += jnp.where(lane >= shift, got, 0.0)
+            sum_ref[b + 1] += jnp.where(lane < shift, got, 0.0)
         return 0
 
     lax.fori_loop(0, levels // per, body, 0)
     for b in range(packed_ref.shape[0]):
-        packed_ref[b] = sum_ref[b].astype(BF)
+        packed_ref[b] = ((sums[0][b] + sums[1][b]) + (sums[2][b] + sums[3][b])).astype(BF)
     copy.wait()
 
 
@@ -214,12 +212,6 @@
             s_ref[...] = s_ref[...] - tn(low, high)[:size]
 
 
-def stacked(a_ref, x, rows):
-    piece = 128 if rows % 128 == 0 else rows
-    parts = [nn(a_ref[r : r + piece], x) + nn(a_ref[rows + r : rows + r + piece], x) for r in range(0, rows, piece)]
-    return jnp.concatenate(parts, axis=0) if len(parts) > 1 else parts[0]
-
-
 def forward_loop(group, c_ref, e_ref, kf_ref, lf_ref, inc_ref, outer_ref, first, last):
     rows, lanes = inc_ref.shape
     ext = rows + outer_ref.shape[1]
@@ -231,7 +223,7 @@
             for m in at:
                 x = c_ref[m]
                 smooth.append(nn(jnp.concatenate([x, x], axis=1), lf_ref[...]).astype(BF))
-            out = [stacked(kf_ref, jnp.concatenate(smooth[2 * i : 2 * i + 2], axis=1), ext) for i in range(2)]
+            out = [nn(kf_ref[...], jnp.concatenate(smooth[2 * i : 2 * i + 2], axis=1)) for i in range(2)]
             total = inc_ref[...]
             for i, m in enumerate(at):
                 part = out[i // 2][:, i % 2 * lanes : (i % 2 + 1) * lanes]
@@ -247,8 +239,8 @@
                     start_ref,
                     p_ref, px_ref, ext_ref, edge_ref, upper_ref,
                     got_left, got_right, got_meta, got_start, start_smem, own_c, own_e, lat_c, lat_e, lat_x, own_x, outer_ref,
-                    inc_ref, wide_ref, send_inc, got_inc, p_edge, got_edge, gram_in, total_ref, given_ref,
-                    far_sem, far_recv, lat_sem, lat_recv, x_sem, x_recv, inc_sem, inc_recv,
+                    inc_ref, wide_ref, send_part, got_part, send_give, got_give, p_edge, got_edge, gram_in, total_ref,
+                    far_sem, far_recv, lat_sem, lat_recv, x_sem, x_recv, inc_sem, inc_recv, give_sem, give_recv,
                     pe_sem, pe_recv, gram_sem, gram_recv, smem_sem):
     levels, cols, lanes = dims
     n_lat, n_lon = sizes
@@ -287,10 +279,12 @@
         greet({axis: flip(lat if axis == "lat" else lon, bit)})
 
     packed_at = iota((rows, lanes), 1) // 4
-    for g in range(groups):
-        first, last = g * per, min((g + 1) * per, members)
-        for ref, own in ((c_ref, own_c), (e_ref, own_e)):
-            def pack(k, x, first=first, ref=ref):
+
+    def pack_edges(ref, own):
+        for g in range(groups):
+            first, last = g * per, min((g + 1) * per, members)
+
+            def pack(k, x, first=first):
                 for i in range(4):
                     m = first + 4 * k + i
                     x = jnp.where(packed_at == m - first, pltpu.roll(ref[m], 2 + 4 * (m - first), 1), x)
@@ -298,6 +292,7 @@
 
             own[g] = lax.fori_loop(0, (last - first) // 4, pack, jnp.zeros((rows, lanes), BF))
 
+    pack_edges(c_ref, own_c)
     pl.semaphore_wait(barrier, 2 + len(partners) + has_before.astype(jnp.int32) + has_after.astype(jnp.int32))
 
     def remote(src, dst, s, r, where):
@@ -330,12 +325,14 @@
         pl.when(has_before)(up.wait_recv)
         pl.when(has_after)(down.wait_recv)
 
-    near = [lat_pair(own_c, lat_c, lat_sem, lat_recv, 0), lat_pair(own_e, lat_e, lat_sem, lat_recv, 1)]
-    for pair in near:
-        lat_start(*pair)
     for copies in far:
-        for copy in copies:
+        for copy in copies[:2]:
             copy.start()
+    for copies in far:
+        copies[2].start()
+    near = lat_pair(own_c, lat_c, lat_sem, lat_recv, 0)
+    lat_start(*near)
+    pack_edges(e_ref, own_e)
 
     for side, missing in ((0, jnp.logical_not(has_before)), (1, jnp.logical_not(has_after))):
         @pl.when(missing)
@@ -344,7 +341,7 @@
                 ref[side] = jnp.zeros_like(ref[side])
 
     for slot in range(2):
-        got[slot][blocks] = jnp.zeros_like(got[slot][blocks])
+        got[slot][blocks:] = jnp.zeros_like(got[slot][blocks:])
     inc_ref[...] = jnp.zeros_like(inc_ref)
 
     two = 2
@@ -376,7 +373,7 @@
     total_ref[...] = jnp.zeros_like(total_ref)
     total_ref[:, :members] = gram[:members] + gram[members:]
 
-    stages = []
+    stages, ended = [], []
 
     def stage_start():
         i = len(stages)
@@ -389,26 +386,29 @@
             stages.append(copy)
 
     def stage_end():
-        i = len(stages) - 1
-        stages[i].wait()
-        total_ref[...] = total_ref[...] + gram_in[i, 1]
+        if len(ended) < len(stages):
+            i = len(ended)
+            stages[i].wait()
+            total_ref[...] = total_ref[...] + gram_in[i, 1]
+            ended.append(i)
 
     group = 8 if members % 8 == 0 else 4
-    cuts = [members // group * i // (n_near + 1) for i in range(n_near + 2)]
+    turns = members // group
+    cuts = [min(2 * i, turns) for i in range(n_near + 1)] + [turns]
     for i in range(n_near + 1):
         stage_start()
         forward_loop(group, c_ref, e_ref, kf_ref, lf_ref, inc_ref, outer_ref, cuts[i], cuts[i + 1])
         if i < n_near:
             stage_end()
 
-    for pair in near:
-        lat_wait(*pair)
+    lat_wait(*near)
+    near_e = lat_pair(own_e, lat_e, lat_sem, lat_recv, 1)
+    lat_start(*near_e)
     before = iota((rows, lanes), 1) % 4 < 2
     spare = []
     for g in range(groups):
         halo = jnp.where(before, lat_c[0, g].astype(F32), lat_c[1, g].astype(F32)).astype(BF)
-        mixed = nn(kf_ref[...], halo)
-        mixed = (mixed[:ext] + mixed[ext:]).astype(BF)
+        mixed = nn(kf_ref[...], halo).astype(BF)
         spare.append(nn(jnp.concatenate([mixed, mixed], axis=1), bf_ref[...]))
     source = iota((lanes, lanes), 0) % 4
     target = iota((lanes, lanes), 1)
@@ -423,68 +423,71 @@
 
     inc_ref[...] += settle([own_e[g].astype(F32) * spare[g][:rows] for g in range(groups)])
 
-    pitch_x = 2 * half + 8
+    for d in range(2):
+        at = slice(d * levels, (d + 1) * levels)
+        send_part[0, at] = inc_ref[pl.ds(cols - 2 + d, levels, stride=cols), :]
+        send_part[1, at] = inc_ref[pl.ds(d, levels, stride=cols), :]
+    swap = []
+    for slot, to in ((0, right), (1, left)):
+        swap.append(remote(send_part.at[slot], got_part.at[slot], inc_sem.at[slot], inc_recv.at[slot], {"lon": to}))
+        swap[-1].start()
+
+    local = []
     for slot in range(2):
-        for copy in far[slot]:
+        for copy in far[slot][:2]:
             copy.wait()
-        copy = pltpu.make_async_copy(got_start.at[slot], start_smem.at[slot], smem_sem)
-        copy.start()
+        local.append(pltpu.make_async_copy(got_start.at[slot], start_smem.at[slot], smem_sem.at[slot]))
+        local[-1].start()
+    for copy in local:
         copy.wait()
+    pitch_x = half + 8
+    for slot in range(2):
+        far[slot][2].wait()
 
         def expand(k, _, slot=slot):
             for i in range(8):
                 h = k * 8 + i
-                b = start_smem[slot, 0, (1 - slot) * half + h]
-                hot = spot(got_meta[slot, 0, pl.ds(h, 1), :], 2 * lanes)
+                start = start_smem[slot, 0, (1 - slot) * half + h]
+                b = start // lanes
+                shift = (start - b * lanes).astype(F32)
+                hot = spot(got_meta[slot, 0, pl.ds(h, 1), :] + shift, 2 * lanes)
                 x = nn(jnp.concatenate([got[slot][b], got[slot][b + 1]], axis=1), hot)
-                wide_ref[pl.ds(slot * half + h, members, stride=pitch_x), :] = x
+                wide_ref[pl.ds(h, members, stride=pitch_x), :] = x
             return 0
 
         lax.fori_loop(0, half // 8, expand, 0)
         if len(stages) > n_near:
             stage_end()
             stage_start()
-
-    given_ref[...] = jnp.zeros_like(given_ref)
-    for g in range(groups):
-        first, last = g * per, min((g + 1) * per, members)
-
-        def outer(k, carry, first=first):
-            total, edges = carry
-            for i in range(4):
-                m = first + 4 * k + i
-                x = wide_ref[pl.ds(pl.multiple_of(m * pitch_x, 8), 2 * half), :]
-                xb = x.astype(BF)
-                ext_ref[m] = xb
-                total = total + x * outer_ref[m].astype(F32)
-                edges = jnp.where(packed_at[: 2 * half] == m - first, pltpu.roll(xb, 2 + 4 * (m - first), 1), edges)
-            return total, edges
-
-        zero = jnp.zeros((2 * half, lanes), F32)
-        total, edges = lax.fori_loop(0, (last - first) // 4, outer, (zero, zero.astype(BF)))
-        given_ref[...] += total
-        own_x[g] = edges
-    given_ref[...] += settle([own_x[g].astype(F32) * spare[g][rows:] for g in range(groups)])
-
-    for d in range(2):
-        at = slice(d * levels, (d + 1) * levels)
-        send_inc[0, 0, at] = inc_ref[pl.ds(cols - 2 + d, levels, stride=cols), :]
-        send_inc[1, 0, at] = inc_ref[pl.ds(d, levels, stride=cols), :]
-    send_inc[0, 1] = given_ref[half:]
-    send_inc[1, 1] = given_ref[:half]
-    swap = []
-    for slot, to in ((0, right), (1, left)):
-        swap.append(remote(send_inc.at[slot], got_inc.at[slot], inc_sem.at[slot], inc_recv.at[slot], {"lon": to}))
-    for copy in swap:
-        copy.start()
+        at_x = slice(slot * half, (slot + 1) * half)
+        given = jnp.zeros((half, lanes), F32)
+        for g in range(groups):
+            first, last = g * per, min((g + 1) * per, members)
+
+            def outer(k, carry, first=first, at_x=at_x):
+                total, edges = carry
+                for i in range(group):
+                    m = first + group * k + i
+                    x = wide_ref[pl.ds(pl.multiple_of(m * pitch_x, 8), half), :]
+                    xb = x.astype(BF)
+                    ext_ref[m, at_x] = xb
+                    total = total + x * outer_ref[m, at_x].astype(F32)
+                    edges = jnp.where(packed_at[:half] == m - first, pltpu.roll(xb, 2 + 4 * (m - first), 1), edges)
+                return total, edges
+
+            given, edges = lax.fori_loop(0, (last - first) // group, outer, (given, jnp.zeros((half, lanes), BF)))
+            own_x[g, at_x] = edges
+        from_row = rows + slot * half
+        send_give[slot] = given + settle(
+            [own_x[g, at_x].astype(F32) * spare[g][from_row : from_row + half] for g in range(groups)])
+        swap.append(remote(send_give.at[slot], got_give.at[1 - slot], give_sem.at[slot], give_recv.at[1 - slot],
+                           {"lon": (left, right)[slot]}))
+        swap[-1].start()
     across = lat_pair(own_x, lat_x, x_sem, x_recv, 0)
     lat_start(*across)
 
-    while True:
-        if stages:
-            stage_end()
-        if len(stages) == len(partners):
-            break
+    while len(ended) < len(partners):
+        stage_end()
         stage_start()
     eye = (iota((members, lanes), 0) == iota((members, lanes), 1)).astype(F32)
     total_obs = packed_ref.shape[0] * lanes * n_lat * n_lon
@@ -495,10 +498,10 @@
         copy.wait()
     for slot in range(2):
         px_ref[slot * half : (slot + 1) * half] = (
-            got_meta[slot, 1] * (got_inc[slot, 0] + given_ref[slot * half : (slot + 1) * half]) - got_meta[slot, 2])
+            got_meta[slot, 1] * (got_part[slot] + send_give[slot]) - got_meta[slot, 2])
         for d in range(2):
             at = pl.ds(slot * (cols - 2) + d, levels, stride=cols)
-            inc_ref[at, :] = inc_ref[at, :] + got_inc[slot, 1, d * levels : (d + 1) * levels]
+            inc_ref[at, :] = inc_ref[at, :] + got_give[slot, d * levels : (d + 1) * levels]
     p_ref[...] = q_ref[...] * inc_ref[...] - v_ref[...]
 
     edge_row, edge_lane = iota((8, lanes), 0), iota((8, lanes), 1)
@@ -507,6 +510,7 @@
     for ref, at in ((p_ref, slice(0, rows)), (px_ref, slice(rows, ext))):
         hi, lo = split(ref[...])
         p_edge[:, at] = nt(pick, hi) + nt(pick, lo)
+    lat_wait(*near_e)
     final = lat_pair(p_edge, got_edge, pe_sem, pe_recv, 0)
     lat_start(*final)
     lat_wait(*across)
@@ -535,8 +539,7 @@
     def _():
         upper_out[...] = upper_ref[...]
         for g in range(edge_ref.shape[0]):
-            z = nn(ka_ref[...], pe_ref[g])
-            z = (z[:rows] + z[rows:]).astype(BF)
+            z = nn(ka_ref[...], pe_ref[g]).astype(BF)
             edge_ref[g] = nn(jnp.concatenate([z, z], axis=1), ba_ref[...])
 
     lane = iota((rows, lanes), 1)
@@ -550,7 +553,7 @@
             own = (e_ref[m].astype(F32) * p).astype(BF)
             far = (ext_ref[m].astype(F32) * px).astype(BF)
             wide.append(jnp.concatenate([own, far], axis=0))
-        mixed = [stacked(ka_ref, jnp.concatenate(wide[2 * i : 2 * i + 2], axis=1), rows).astype(BF) for i in range(2)]
+        mixed = [nn(ka_ref[...], jnp.concatenate(wide[2 * i : 2 * i + 2], axis=1)).astype(BF) for i in range(2)]
         smooth = []
         for i in range(4):
             z = mixed[i // 2][:, i % 2 * lanes : (i % 2 + 1) * lanes]
@@ -585,7 +588,7 @@
         functools.partial(setup_kernel, dims),
         in_specs=[hbm, hbm, sm] + [hbm] * 6,
         out_specs=[vm] * 11,
-        out_shape=[sds((members, rows, lanes), BF), sds((2 * ext, rows), BF), sds((2 * rows, ext), BF)]
+        out_shape=[sds((members, rows, lanes), BF), sds((ext, rows), BF), sds((rows, ext), BF)]
         + [sds((2 * lanes, lanes), BF)] * 4
         + [sds((rows, lanes)), sds((rows, lanes)), sds((2, 3, half, lanes)), sds((8, 2 * half), jnp.int32)],
         scratch_shapes=[pltpu.VMEM((levels, levels), BF), pltpu.VMEM((1, slots), jnp.int32),
@@ -602,7 +605,7 @@
         out_specs=[vm] * 2,
         out_shape=[sds((members, rows, lanes), BF), sds((blocks, members, lanes), BF)],
         scratch_shapes=[pltpu.VMEM((members * (4 * cols + 8), lanes), F32),
-                        pltpu.VMEM((blocks + 1, members, lanes), F32), dma],
+                        *[pltpu.VMEM((blocks + 2, members, lanes), F32)] * 4, dma],
         compiler_params=pltpu.CompilerParams(vmem_limit_bytes=8 * MIB),
         name="gather",
     )(start, away(control.reshape(members, rows, lanes)), e3, meta)
@@ -615,8 +618,8 @@
         out_shape=[sds((rows, lanes)), sds((2 * half, lanes)), sds((members, 2 * half, lanes), BF),
                    sds((groups, ext, lanes), BF), sds((members, members))],
         scratch_shapes=[
-            pltpu.VMEM((blocks + 1, members, lanes), BF),
-            pltpu.VMEM((blocks + 1, members, lanes), BF),
+            pltpu.VMEM((blocks + 2, members, lanes), BF),
+            pltpu.VMEM((blocks + 2, members, lanes), BF),
             pltpu.VMEM((2, 3, half, lanes), F32),
             pltpu.VMEM((2, 8, 2 * half), jnp.int32),
             pltpu.SMEM((2, 8, 2 * half), jnp.int32),
@@ -628,23 +631,25 @@
             pltpu.VMEM((groups, 2 * half, lanes), BF),
             pltpu.VMEM((members, 2 * half, lanes), BF),
             pltpu.VMEM((rows, lanes), F32),
-            pltpu.VMEM((members * (2 * half + 8), lanes), F32),
-            pltpu.VMEM((2, 2, half, lanes), F32),
-            pltpu.VMEM((2, 2, half, lanes), F32),
+            pltpu.VMEM((members * max(half, 2 * cols) + 8 * members, lanes), F32),
+            pltpu.VMEM((2, half, lanes), F32),
+            pltpu.VMEM((2, half, lanes), F32),
+            pltpu.VMEM((2, half, lanes), F32),
+            pltpu.VMEM((2, half, lanes), F32),
             pltpu.VMEM((8, ext), F32),
             pltpu.VMEM((2, 8, ext), F32),
             pltpu.VMEM((n_bits, 2, members, lanes), F32),
             pltpu.VMEM((members, lanes), F32),
-            pltpu.VMEM((2 * half, lanes), F32),
             dma((2, 3)), dma((2, 3)), dma((2, 2)), dma((2, 2)), dma((2, 1)), dma((2, 1)), dma((2,)), dma((2,)),
-            dma((2, 1)), dma((2, 1)), dma((n_bits,)), dma((n_bits,)), dma,
+            dma((2,)), dma((2,)),
+            dma((2, 1)), dma((2, 1)), dma((n_bits,)), dma((n_bits,)), dma((2,)),
         ],
         compiler_params=pltpu.CompilerParams(
             vmem_limit_bytes=16 * MIB, collective_id=0, has_side_effects=True),
         name="exchange",
     )(c3, e3, q, v, kf, lf, bf, packed, meta, start)
 
-    block = 8 if members % 8 == 0 else 4
+    block = next(b for b in (BLOCK, 8, 4) if members % b == 0)
     gradient, upper = pl.pallas_call(
         functools.partial(adjoint_kernel, dims, block),
         grid=(members // block,),

time: 67.4 us -> 63.3 us (0.939)
  Pallas kernels: 65.9 us -> 61.8 us
    pallas_call x1, Pallas kernels: 13.1 us -> 10.5 us  [shards(): pl.pallas_call(functools.partial(adjoint_kernel, dims, block), grid=(memb...]
    pallas_call x1, Pallas kernels: 44.6 us -> 42.9 us  [shards(): pl.pallas_call(functools.partial(exchange_kernel, dims, (n_lat, n_lon)),...]
where the time goes in v4:
time: 63.3 us; the launch traced here: 63.1 us
  Pallas kernels  61.8 us (98%)
  between operations  1.3 us (2%)
    pallas_call x1, Pallas kernels, shards(): pl.pallas_call(functools.partial(exchange_kernel, dims, (n_lat, n_lon)),...  42.9 us
    pallas_call x1, Pallas kernels, shards(): pl.pallas_call(functools.partial(adjoint_kernel, dims, block), grid=(memb...  10.5 us
    pallas_call x1, Pallas kernels, shards(): pl.pallas_call(functools.partial(gather_kernel, dims), in_specs=[sm, hbm,...  5.63 us
    pallas_call x1, Pallas kernels, shards(): pl.pallas_call(functools.partial(setup_kernel, dims), in_specs=[hbm, hbm,...  2.8 us

profile of v4, /device:TPU:1, one launch (start us, length us, event | category | flops | bytes accessed | tf_op | source)
XLA Modules:
  0.0 63.1 jit_solution(8967391544484545045)
XLA Ops:
  1.3 2.8 %setup.1 = (bf16[80,256,128]{2,1,0:T(8,128)(2,1)S(1)}, bf16[384,256]{1,0:T(8,128)(2,1)S(1)}, bf16[256,384]{1,0:T(8,128)(2,1)S(1)}, bf16[256,128]{1,0:T(8,128)(2,...) custom-call(f32[4]{0:T(128)} %lat_hbm.1, ...), custom_call_target="tpu_custom_call" | custom-call | tf_op jit(solution)/shard_map/setup/pallas_call | solution.py:587
  4.1 5.6 %gather.1 = (bf16[80,256,128]{2,1,0:T(8,128)(2,1)S(1)}, bf16[16,80,128]{2,1,0:T(8,128)(2,1)S(1)}) custom-call(s32[8,128]{1,0:T(8,128)S(1)} %get-tuple-element.22.start_ref, bf16[80,256,128]{2,1,0:T(8,128)(2,1)} %bitcast.8, bf16[80,256,128]{2,1,0:T(8,128)(2,1)S(1)} %get-tuple-element.23.e_ref, f32[2,3,64,128]{3,2,1,0:T(8,128)S(1)} %get-tuple-element.24.meta_ref), custom_call_target="tpu_custom_call" | custom-call | tf_op jit(solution)/shard_map/gather/pallas_call | solution.py:602
  9.7 42.9 %exchange.1 = (f32[256,128]{1,0:T(8,128)S(1)}, f32[128,128]{1,0:T(8,128)S(1)}, bf16[80,128,128]{2,1,0:T(8,128)(2,1)S(1)}, bf16[3,384,128]{2,1,0:T(8,128)(2,1)S(1)}, f32[80,80]{1,0:T(8,128)S(1)}) custom-call(bf16[80,256,128]{2,1,0:T(8,128)(2,1)S(1)} %get-tuple-element.25.c_ref, bf16[80,256,128]{2,1,0:T(8,128)(2,1)S(1)} %get-tuple-element.23.e_ref, ...), custom_call_target="tpu_custom_call" | custom-call | tf_op jit(solution)/shard_map/exchange/pallas_call | solution.py:614
  52.6 10.5 %adjoint.1 = (f32[80,256,128]{2,1,0:T(8,128)}, f32[80,80]{1,0:T(8,128)}) custom-call(bf16[80,256,128]{2,1,0:T(8,128)(2,1)S(1)} %get-tuple-element.25.c_ref, bf16[80,256,128]{2,1,0:T(8,128)(2,1)S(1)} %get-tuple-element.23.e_ref, bf16[80,128,128]{2,1,0:T(8,128)(2,1)S(1)} %get-tuple-element.32.ext_ref, f32[256,128]{1,0:T(8,128)S(1)} %get-tuple-element.33.p_ref, ...), custom_call_target="tpu_custom_call" | custom-call | tf_op jit(solution)/shard_map/adjoint/pallas_call | solution.py:653

commit v5 on v4

--- a/solution.py
+++ b/solution.py
@@ -11,6 +11,7 @@
 F32, BF = jnp.float32, jnp.bfloat16
 MIB = 1024 * 1024
 BLOCK = 16
+LARGE = 4
 MESH = pl.DeviceIdType.MESH
 
 
@@ -56,10 +57,11 @@
     small = [pltpu.make_async_copy(a, b, sems.at[i]) for i, (a, b) in enumerate(
         ((mix_hbm, mix_ref), (place_hbm, place_ref), (keep_hbm, keep_ref), (weight_hbm, weight_ref),
          (innov_hbm, innov_ref), (lat_hbm, lat_taps), (lon_hbm, lon_taps)))]
-    large = pltpu.make_async_copy(e_hbm, e_ref, sems.at[len(small)])
-    for copy in small:
+    part = e_ref.shape[0] // LARGE
+    large = [pltpu.make_async_copy(e_hbm.at[pl.ds(i * part, part)], e_ref.at[pl.ds(i * part, part)],
+                                   sems.at[len(small) + i]) for i in range(LARGE)]
+    for copy in small + large:
         copy.start()
-    large.start()
     for copy in small:
         copy.wait()
     rows, half = levels * cols, 2 * levels
@@ -131,7 +133,8 @@
         meta_ref[side, 0] = relative[at]
         meta_ref[side, 1] = q[rows:][at]
         meta_ref[side, 2] = v[rows:][at]
-    large.wait()
+    for copy in large:
+        copy.wait()
 
 
 def spot(relative_row, width):
@@ -144,13 +147,13 @@
     return ref[pl.ds(j, members, stride=stride), :]
 
 
-def gather_kernel(dims, start_ref, c_hbm, e_ref, meta_ref, c_ref, packed_ref, wide_ref, *rest):
+def gather_kernel(dims, start_ref, c_hbm, e_ref, meta_ref, c_ref, packed_ref, wide_a, wide_b, sum_a, sum_b, sem):
     levels, cols, lanes = dims
     members = e_ref.shape[0]
     half = 2 * levels
     per = 4
     pitch = per * cols + 8
-    sums, sem = rest[:4], rest[4]
+    wide, sums = (wide_a, wide_b), (sum_a, sum_b)
     copy = pltpu.make_async_copy(c_hbm, c_ref, sem)
     copy.start()
     for ref in sums:
@@ -158,31 +161,33 @@
     lane = iota((members, lanes), 1)
 
     def body(g, _):
-        base = pl.multiple_of(g * per * cols, per * cols)
-        x = e_ref[:, pl.ds(base, per * cols), :].astype(F32)
-        for m in range(members):
-            wide_ref[m * pitch : m * pitch + per * cols, :] = x[m]
-        found = []
-        for j in range(per * cols):
-            col = j % cols
-            if 2 <= col < cols - 2:
-                continue
-            side = int(col >= 2)
-            h = (col - side * (cols - 2)) * levels + g * per + j // cols
-            xb = load_rows(wide_ref, j, members, pitch).astype(BF)
-            got = nt(xb, spot(meta_ref[side, 0, pl.ds(h, 1), :], lanes))
-            first = start_ref[0, side * half + h]
-            b = first // lanes
-            found.append((sums[2 * side + col - side * (cols - 2)], b, first - b * lanes, got))
-        for sum_ref, b, shift, got in found:
-            got = pltpu.roll(got, shift, 1)
-            sum_ref[b] += jnp.where(lane >= shift, got, 0.0)
-            sum_ref[b + 1] += jnp.where(lane < shift, got, 0.0)
+        for k in range(2):
+            base = pl.multiple_of((2 * g + k) * per * cols, per * cols)
+            x = e_ref[:, pl.ds(base, per * cols), :].astype(F32)
+            for m in range(members):
+                wide[k][m * pitch : m * pitch + per * cols, :] = x[m]
+        for k in range(2):
+            found = []
+            for j in range(per * cols):
+                col = j % cols
+                if 2 <= col < cols - 2:
+                    continue
+                side = int(col >= 2)
+                h = (col - side * (cols - 2)) * levels + (2 * g + k) * per + j // cols
+                xb = load_rows(wide[k], j, members, pitch).astype(BF)
+                got = nt(xb, spot(meta_ref[side, 0, pl.ds(h, 1), :], lanes))
+                first = start_ref[0, side * half + h]
+                b = first // lanes
+                found.append((sums[side], b, first - b * lanes, got))
+            for ref, b, shift, got in found:
+                got = pltpu.roll(got, shift, 1)
+                ref[b] += jnp.where(lane >= shift, got, 0.0)
+                ref[b + 1] += jnp.where(lane < shift, got, 0.0)
         return 0
 
-    lax.fori_loop(0, levels // per, body, 0)
+    lax.fori_loop(0, levels // (2 * per), body, 0)
     for b in range(packed_ref.shape[0]):
-        packed_ref[b] = ((sums[0][b] + sums[1][b]) + (sums[2][b] + sums[3][b])).astype(BF)
+        packed_ref[b] = (sum_a[b] + sum_b[b]).astype(BF)
     copy.wait()
 
 
@@ -328,11 +333,20 @@
     for copies in far:
         for copy in copies[:2]:
             copy.start()
-    for copies in far:
-        copies[2].start()
+    wraps_left = lon == 0
+
+    @pl.when(wraps_left)
+    def _():
+        far[1][2].start()
+        far[0][2].start()
+
+    @pl.when(jnp.logical_not(wraps_left))
+    def _():
+        far[0][2].start()
+        far[1][2].start()
+
     near = lat_pair(own_c, lat_c, lat_sem, lat_recv, 0)
     lat_start(*near)
-    pack_edges(e_ref, own_e)
 
     for side, missing in ((0, jnp.logical_not(has_before)), (1, jnp.logical_not(has_after))):
         @pl.when(missing)
@@ -393,11 +407,14 @@
             ended.append(i)
 
     group = 8 if members % 8 == 0 else 4
-    turns = members // group
-    cuts = [min(2 * i, turns) for i in range(n_near + 1)] + [turns]
+    span = 16 if members % 16 == 0 else group
+    turns = members // span
+    cuts = [0, 0] + [min(i, turns) for i in range(1, n_near)] + [turns] if n_near else [0, turns]
     for i in range(n_near + 1):
         stage_start()
-        forward_loop(group, c_ref, e_ref, kf_ref, lf_ref, inc_ref, outer_ref, cuts[i], cuts[i + 1])
+        if i == 0:
+            pack_edges(e_ref, own_e)
+        forward_loop(span, c_ref, e_ref, kf_ref, lf_ref, inc_ref, outer_ref, cuts[i], cuts[i + 1])
         if i < n_near:
             stage_end()
 
@@ -593,7 +610,7 @@
         + [sds((rows, lanes)), sds((rows, lanes)), sds((2, 3, half, lanes)), sds((8, 2 * half), jnp.int32)],
         scratch_shapes=[pltpu.VMEM((levels, levels), BF), pltpu.VMEM((1, slots), jnp.int32),
                         pltpu.VMEM((1, slots), jnp.int32), pltpu.VMEM((1, slots), F32), pltpu.VMEM((1, slots), F32),
-                        pltpu.SMEM((4,), F32), pltpu.SMEM((4,), F32), dma((8,))],
+                        pltpu.SMEM((4,), F32), pltpu.SMEM((4,), F32), dma((7 + LARGE,))],
         compiler_params=pltpu.CompilerParams(vmem_limit_bytes=8 * MIB),
         name="setup",
     )(away(lat_taps), away(lon_taps), obs_count, away(ensemble.reshape(members, rows, lanes)), away(level_mix),
@@ -604,8 +621,8 @@
         in_specs=[sm, hbm, vm, vm],
         out_specs=[vm] * 2,
         out_shape=[sds((members, rows, lanes), BF), sds((blocks, members, lanes), BF)],
-        scratch_shapes=[pltpu.VMEM((members * (4 * cols + 8), lanes), F32),
-                        *[pltpu.VMEM((blocks + 2, members, lanes), F32)] * 4, dma],
+        scratch_shapes=[*[pltpu.VMEM((members * (4 * cols + 8), lanes), F32)] * 2,
+                        *[pltpu.VMEM((blocks + 2, members, lanes), F32)] * 2, dma],
         compiler_params=pltpu.CompilerParams(vmem_limit_bytes=8 * MIB),
         name="gather",
     )(start, away(control.reshape(members, rows, lanes)), e3, meta)

time: 63.3 us -> 62 us (0.979)
  Pallas kernels: 61.8 us -> 60.5 us
    pallas_call x1, Pallas kernels: 5.63 us -> 4.87 us  [shards(): pl.pallas_call(functools.partial(gather_kernel, dims), in_specs=[sm, hbm,...]
where the time goes in v5:
time: 62 us; the launch traced here: 61.8 us
  Pallas kernels  60.5 us (98%)
  between operations  1.3 us (2%)
    pallas_call x1, Pallas kernels, shards(): pl.pallas_call(functools.partial(exchange_kernel, dims, (n_lat, n_lon)),...  42.3 us
    pallas_call x1, Pallas kernels, shards(): pl.pallas_call(functools.partial(adjoint_kernel, dims, block), grid=(memb...  10.5 us
    pallas_call x1, Pallas kernels, shards(): pl.pallas_call(functools.partial(gather_kernel, dims), in_specs=[sm, hbm,...  4.87 us
    pallas_call x1, Pallas kernels, shards(): pl.pallas_call(functools.partial(setup_kernel, dims), in_specs=[hbm, hbm,...  2.83 us

profile of v5, /device:TPU:1, one launch (start us, length us, event | category | flops | bytes accessed | tf_op | source)
XLA Modules:
  0.0 61.8 jit_solution(16343187691294485590)
XLA Ops:
  1.3 2.8 %setup.1 = (bf16[80,256,128]{2,1,0:T(8,128)(2,1)S(1)}, bf16[384,256]{1,0:T(8,128)(2,1)S(1)}, bf16[256,384]{1,0:T(8,128)(2,1)S(1)}, bf16[256,128]{1,0:T(8,128)(2,...) custom-call(f32[4]{0:T(128)} %lat_hbm.1, ...), custom_call_target="tpu_custom_call" | custom-call | tf_op jit(solution)/shard_map/setup/pallas_call | solution.py:604
  4.1 4.9 %gather.1 = (bf16[80,256,128]{2,1,0:T(8,128)(2,1)S(1)}, bf16[16,80,128]{2,1,0:T(8,128)(2,1)S(1)}) custom-call(s32[8,128]{1,0:T(8,128)S(1)} %get-tuple-element.22.start_ref, bf16[80,256,128]{2,1,0:T(8,128)(2,1)} %bitcast.8, bf16[80,256,128]{2,1,0:T(8,128)(2,1)S(1)} %get-tuple-element.23.e_ref, f32[2,3,64,128]{3,2,1,0:T(8,128)S(1)} %get-tuple-element.24.meta_ref), custom_call_target="tpu_custom_call" | custom-call | tf_op jit(solution)/shard_map/gather/pallas_call | solution.py:619
  9.0 42.3 %exchange.1 = (f32[256,128]{1,0:T(8,128)S(1)}, f32[128,128]{1,0:T(8,128)S(1)}, bf16[80,128,128]{2,1,0:T(8,128)(2,1)S(1)}, bf16[3,384,128]{2,1,0:T(8,128)(2,1)S(1)}, f32[80,80]{1,0:T(8,128)S(1)}) custom-call(bf16[80,256,128]{2,1,0:T(8,128)(2,1)S(1)} %get-tuple-element.25.c_ref, bf16[80,256,128]{2,1,0:T(8,128)(2,1)S(1)} %get-tuple-element.23.e_ref, ...), custom_call_target="tpu_custom_call" | custom-call | tf_op jit(solution)/shard_map/exchange/pallas_call | solution.py:631
  51.3 10.5 %adjoint.1 = (f32[80,256,128]{2,1,0:T(8,128)}, f32[80,80]{1,0:T(8,128)}) custom-call(bf16[80,256,128]{2,1,0:T(8,128)(2,1)S(1)} %get-tuple-element.25.c_ref, bf16[80,256,128]{2,1,0:T(8,128)(2,1)S(1)} %get-tuple-element.23.e_ref, bf16[80,128,128]{2,1,0:T(8,128)(2,1)S(1)} %get-tuple-element.32.ext_ref, f32[256,128]{1,0:T(8,128)S(1)} %get-tuple-element.33.p_ref, ...), custom_call_target="tpu_custom_call" | custom-call | tf_op jit(solution)/shard_map/adjoint/pallas_call | solution.py:670
